TPU v7x, 128 devices: a whole 4x4x4 slice. The times are simulated.
128 devices in a mesh: rcv: 16 (over x_hi, y, core), src: 8 (over z, x_lo).
Axes of the slice: x: 4 (x_hi: 2, x_lo: 2; x = x_hi * 2 + x_lo), y: 4, z: 4, core: 2. Of those that a mesh axis runs over, the one named last changes fastest.
Arguments:
- kernel_codes: bfloat16 [2, 8192, 65536], P(None, 'rcv', 'src'), may hold values from -128 to 127
- kernel_exps: int32 [8192, 512], P('rcv', 'src'), may hold values from -17 to -14
- wavefield: bfloat16 [2, 65536, 128], P(None, 'src', 'rcv'), may hold values from -6 to 6
- observed: bfloat16 [2, 8192, 128], P(None, 'rcv'), may hold values from -6 to 6
- receiver_mask: int32 [8192], P('rcv'), may hold values 0 or 1
Outputs:
- residual: bfloat16 [2, 8192, 128], P(None, 'rcv', 'src')
- gradient: bfloat16 [2, 65536, 128], P(None, 'src', 'rcv')
All inputs are finite; a program needn't handle non-finite values. No bound on the sum of `receiver_mask` on one device may be relied on, other than what follows from the above.
Results may differ from a plain program's by a relative error of at most 0.0049.
Values may be sent and summed in bfloat16 or wider, within the bound.
No kernel may reach another device: no remote copies, remote signals or barrier semaphores. Data moves between devices by JAX's collectives and lax.ppermute only.
A program may use at most 128 MiB of HBM per device.

v0:
```python
import jax
import jax.numpy as jnp
from jax import lax
from jax.sharding import PartitionSpec as P

EXP_BLOCK = 128


def decode(codes, exps):
    rows = codes.shape[1]
    cols = codes.shape[2]
    scale = jnp.exp2(exps.astype(jnp.float32))[:, :, None]

    def widen(values):
        blocks = values.reshape(rows, cols // EXP_BLOCK, EXP_BLOCK).astype(jnp.float32) * scale
        return blocks.reshape(rows, cols).astype(jnp.bfloat16)

    return jnp.concatenate([widen(codes[0]), widen(codes[1])], axis=0)


def body(kernel_codes, kernel_exps, wavefield, observed, receiver_mask):
    rows = kernel_codes.shape[1]
    n_src = lax.axis_size("src")
    stacked = decode(kernel_codes, kernel_exps)
    piece = lax.all_gather(wavefield, "rcv", axis=2, tiled=True)
    span = piece.shape[2]
    joined = jnp.concatenate([piece[0], piece[1]], axis=1)
    prod = jnp.dot(stacked, joined, preferred_element_type=jnp.float32)
    pred_real = prod[:rows, :span] - prod[rows:, span:]
    pred_imag = prod[:rows, span:] + prod[rows:, :span]
    partial_pred = jnp.stack([pred_real, pred_imag])
    width = partial_pred.shape[2]
    share_cols = width // n_src
    live = receiver_mask.astype(jnp.float32)[None, :, None]
    predicted = lax.psum(partial_pred, "src")
    resid = (live * (predicted - observed.astype(jnp.float32))).astype(jnp.bfloat16)
    own_resid = lax.dynamic_slice_in_dim(resid, lax.axis_index("src") * share_cols, share_cols, 2)
    left = jnp.concatenate([resid[0], resid[1]], axis=0)
    right = jnp.concatenate([resid[1], -resid[0]], axis=0)
    grad_real = lax.dot_general(
        stacked, left, (((0,), (0,)), ((), ())), preferred_element_type=jnp.float32
    )
    grad_imag = lax.dot_general(
        stacked, right, (((0,), (0,)), ((), ())), preferred_element_type=jnp.float32
    )
    summed = lax.psum_scatter(
        jnp.stack([grad_real, grad_imag]), "rcv", scatter_dimension=2, tiled=True
    )
    gradient = summed.astype(jnp.bfloat16)
    return (own_resid, gradient)


def solution(mesh):
    in_specs = (
        P(None, "rcv", "src"),
        P("rcv", "src"),
        P(None, "src", "rcv"),
        P(None, "rcv", None),
        P("rcv"),
    )
    out_specs = (P(None, "rcv", "src"), P(None, "src", "rcv"))
    return jax.shard_map(body, mesh=mesh, in_specs=in_specs, out_specs=out_specs, check_vma=False)
```

profile of v0, /device:TPU:0, one launch (start us, length us, event | category | flops | bytes accessed | tf_op | source)
XLA Modules:
  0.0 313.3 jit_solution(1897431621627236321)
XLA Ops:
  7.2 0.0 all-gather.2.cloned.1.call-start
  7.2 0.7 all-gather.2.cloned.1.call-update
  7.9 0.0 all-reduce.4.cloned.1.call-start
  7.9 0.9 multiply_exponential_fusion
  8.9 0.1 copy.10
  9.0 4.6 %mul.30 = f32[512,64,128]{2,1,0:T(8,128)S(1)} broadcast(f32[512,64]{1,0:T(8,128)S(1)} %copy.10), dimensions={0,1} | broadcast | bytes 16908288 | tf_op jit(solution)/shard_map/mul | solution.py:15
  13.6 18.3 %fusion = (bf16[512,8192]{1,0:T(8,128)(2,1)}, bf16[512,8192]{1,0:T(8,128)(2,1)}) fusion(f32[64,8,64,128]{3,2,1,0:T(8,128)S(1)} %bitcast.33, bf16[2,512,8192]{2,1,0:T(8,128)(2,1)} %param.5), kind=kLoop, calls=%fused_computation.2 | loop fusion | flops 25165824 | bytes 50331648 | tf_op jit(solution)/shard_map/convert_element_type | solution.py:16
  32.0 35.8 %all-gather.2.cloned.1.call-done = bf16[2,8192,128]{1,2,0:T(8,128)(2,1)} async-done(((bf16[2,8192,8]{1,2,0:T(8,128)(2,1)}), bf16[2,8192,128]{1,2,0:T(8,128)(2,1)}) %all-gather.2.cloned.1.call-update) | async-done | bytes 4194320 | tf_op jit(solution)/shard_map/all_gather | solution.py:25
  67.7 0.0 copy-start
  67.7 4.1 %slice_bitcast_fusion.1 = (bf16[8192,128]{0,1:T(8,128)(2,1)S(1)}, bf16[8192,128]{0,1:T(8,128)(2,1)}) fusion(bf16[2,8192,128]{1,2,0:T(8,128)(2,1)} %all-gather.2.cloned.1.call-done), kind=kLoop, calls=%fused_computation.13 | loop fusion | bytes 8388608 | tf_op jit(solution)/shard_map/squeeze | solution.py:27
  71.8 1.3 copy-done
  73.1 0.0 copy-start.2
  73.1 0.0 copy-start.3
  73.1 0.0 copy-start.1
  73.1 9.5 %fusion.2 = f32[1024,256]{1,0:T(8,128)} fusion(bf16[512,8192]{1,0:T(8,128)(2,1)} %get-tuple-element.7, bf16[512,8192]{1,0:T(8,128)(2,1)S(1)} %copy-done, bf16[8192,128]{0,1:T(8,128)(2,1)} %get-tuple-element.9, bf16[8192,128]{0,1:T(8,128)(2,1)S(1)} %get-tuple-element.8), kind=kOutput, calls=%fused_computation.8 | convolution fusion | flops 4336910336 | bytes 22020096 | tf_op jit(solution)/shard_map/dot_general | solution.py:28
  82.7 1.2 fusion.7
  83.9 0.8 pad_maximum_fusion.5
  84.7 0.0 all-reduce.4.cloned.1.call-update
  84.8 0.0 copy-done.2
  84.8 0.0 copy-done.3
  84.8 0.6 dynamic-slice
  86.1 73.1 %all-reduce.4.cloned.1.call-done = f32[2,512,128]{2,1,0:T(8,128)} async-done(((f32[2,512,128]{2,1,0:T(8,128)}), f32[2,512,128]{2,1,0:T(8,128)}) %all-reduce.4.cloned.1.call-update) | async-done | bytes 524304 | tf_op jit(solution)/shard_map/psum | solution.py:35
  159.2 0.0 copy-done.1
  159.2 0.0 slice-start
  159.2 0.0 slice-start.2
  159.2 1.3 multiply_convert_fusion
  160.6 0.0 slice-start.1
  160.6 0.0 slice-start.3
  160.6 10.2 %convolution_bitcast_fusion.1 = f32[1,8192,128]{2,1,0:T(8,128)} fusion(bf16[512,8192]{1,0:T(8,128)(2,1)} %get-tuple-element.7, bf16[512,8192]{1,0:T(8,128)(2,1)} %get-tuple-element.6, bf16[512,128]{1,0:T(8,128)(2,1)S(1)} %get-tuple-element.13, bf16[512,128]{1,0:T(8,128)(2,1)S(1)} %get-tuple-element.12), kind=kOutput, calls=%fused_computation.6 | convolution fusion | flops 2181562368 | bytes 21233664 | tf_op jit(solution)/shard_map/dot_general | solution.py:40
  170.8 0.0 slice-done
  170.8 0.0 slice-done.2
  170.9 0.0 slice-done.1
  170.9 0.9 slice-done.3
  171.7 6.3 %convolution_bitcast_fusion = f32[1,8192,128]{2,1,0:T(8,128)} fusion(bf16[512,8192]{1,0:T(8,128)(2,1)S(1)} %bitcast.37, bf16[512,8192]{1,0:T(8,128)(2,1)S(1)} %bitcast.35, bf16[512,128]{1,0:T(8,128)(2,1)S(1)} %fusion.17, bf16[512,128]{1,0:T(8,128)(2,1)S(1)} %get-tuple-element.13), kind=kOutput, calls=%fused_computation.5 | convolution fusion | flops 2181562368 | bytes 21233664 | tf_op jit(solution)/shard_map/dot_general | solution.py:43
  178.0 7.2 %pad_maximum_fusion.1 = f32[2,8192,128]{2,1,0:T(8,128)} fusion(f32[1,8192,128]{2,1,0:T(8,128)} %convolution_bitcast_fusion, f32[1,8192,128]{2,1,0:T(8,128)} %convolution_bitcast_fusion.1), kind=kLoop, calls=%fused_computation.7 | loop fusion | flops 2097152 | bytes 16777216 | tf_op jit(solution)/shard_map/stack | solution.py:47
  185.2 13.2 %copy.11 = f32[2,8192,128]{1,0,2:T(2,128)} copy(f32[2,8192,128]{2,1,0:T(8,128)} %pad_maximum_fusion.1) | data formatting | bytes 16777216 | tf_op jit(solution)/shard_map/stack | solution.py:47
  198.4 105.1 %all-reduce.5 = bf16[2,8192,128]{1,0,2:T(2,128)(2,1)} all-reduce(f32[2,8192,128]{1,0,2:T(2,128)} %copy.11), channel_id=2, replica_groups=mesh['rcv'=16,'src'=8] {'rcv'}, use_global_device_ids=true, to_apply=%region_1.0.clone | all-reduce | flops 2097152 | bytes 12582912
  303.6 1.1 dynamic-slice_convert_fusion
  304.7 0.9 copy.13
  305.6 0.1 constant_dynamic-slice_fusion
  305.7 0.7 copy.12
  (5 shorter events, 0.0 us)
Async XLA Ops:
  7.2 60.6 %all-gather.2.cloned.1.call-start = ((), (), s32[]{:S(2)}) async-start(), calls=%async_computation | async-start | bytes 4456448 | tf_op jit(solution)/shard_map/all_gather | solution.py:25
  7.9 151.3 %all-reduce.4.cloned.1.call-start = ((), (), s32[]{:S(2)}) async-start(), calls=%async_computation.1 | async-start | bytes 1048576 | tf_op jit(solution)/shard_map/psum | solution.py:35
  67.7 5.4 %copy-start = (bf16[512,8192]{1,0:T(8,128)(2,1)S(1)}, bf16[512,8192]{1,0:T(8,128)(2,1)}, u32[]{:S(2)}) copy-start(bf16[512,8192]{1,0:T(8,128)(2,1)} %get-tuple-element.6) | copy-start | bytes 25165828
  73.1 11.7 %copy-start.2 = (s32[512]{0:T(512)S(1)}, s32[512]{0:T(512)}, u32[]{:S(2)}) copy-start(s32[512]{0:T(512)} %param.9) | copy-start | bytes 6148
  73.1 11.7 %copy-start.3 = (u32[128]{0:T(128)S(1)}, u32[128]{0:T(128)}, u32[]{:S(2)}) copy-start(u32[128]{0:T(128)} %constant.15) | copy-start | bytes 1540
  73.1 86.1 %copy-start.1 = (bf16[2,512,128]{2,1,0:T(8,128)(2,1)S(1)}, bf16[2,512,128]{2,1,0:T(8,128)(2,1)}, u32[]{:S(2)}) copy-start(bf16[2,512,128]{2,1,0:T(8,128)(2,1)} %param.8) | copy-start | bytes 786436
  159.2 11.6 %slice-start = ((s8[8388608]{0:T(1024)(128)(4,1)}), s8[4194304]{0:T(1024)(128)(4,1)S(1)}, s32[]{:S(2)}) async-start(s8[8388608]{0:T(1024)(128)(4,1)} %bitcast.34), calls=%async_computation.2 | async-start | bytes 8388608
  159.2 11.6 %slice-start.2 = ((s8[8388608]{0:T(1024)(128)(4,1)}), s8[4194304]{0:T(1024)(128)(4,1)S(1)}, s32[]{:S(2)}) async-start(s8[8388608]{0:T(1024)(128)(4,1)} %bitcast.36), calls=%async_computation.4 | async-start | bytes 8388608
  160.6 10.3 %slice-start.1 = ((s8[8388608]{0:T(1024)(128)(4,1)}), s8[4194304]{0:T(1024)(128)(4,1)S(1)}, s32[]{:S(2)}) async-start(s8[8388608]{0:T(1024)(128)(4,1)} %bitcast.34), calls=%async_computation.3 | async-start | bytes 8388608
  160.6 11.1 %slice-start.3 = ((s8[8388608]{0:T(1024)(128)(4,1)}), s8[4194304]{0:T(1024)(128)(4,1)S(1)}, s32[]{:S(2)}) async-start(s8[8388608]{0:T(1024)(128)(4,1)} %bitcast.36), calls=%async_computation.5 | async-start | bytes 8388608
Sparse Core Ops, SparseCore 0:
  10.5 57.1 all-gather.1
  84.9 74.2 all-reduce.3
where the time goes:
time: 314 us; the launch traced here: 313 us
  waiting for transfers between devices  110 us (35%)
  blocking collectives  105 us (33%)
  other arithmetic  29.9 us (10%)
  local copies, waits for them, and re-layouts  27.7 us (9%)
  matrix products  26 us (8%)
  between operations  14.8 us (5%)
    unnamed x1, blocking collectives  105 us
    psum x1, waiting for transfers between devices, body(): predicted = lax.psum(partial_pred, 'src')  73.1 us
    all_gather x1, waiting for transfers between devices, body(): piece = lax.all_gather(wavefield, 'rcv', axis=2, tiled=True)  35.8 us
    convert_element_type x1, other arithmetic, widen(): return blocks.reshape(rows, cols).astype(jnp.bfloat16)  18.3 us
    another operation x1, local copies, waits for them, and re-layouts, body(): jnp.stack([grad_real, grad_imag])  13.2 us
    dot_general x1, matrix products, body(): lax.dot_general(stacked, left, (((0,), (0,)), ((), ())), preferred_elemen...  10.2 us
    dot_general x1, matrix products, body(): prod = jnp.dot(stacked, joined, preferred_element_type=jnp.float32)  9.54 us
    another operation x1, other arithmetic, body(): jnp.stack([grad_real, grad_imag])  7.24 us
  transfers between devices with their start and end apart: 2, of which 2 were waited for; matrix products, arithmetic and copies ran while one was open for 8% of the time, Pallas kernels for 0%

commit v1 on v0

v1 whole, which is shorter than its diff:
```python
import jax
import jax.numpy as jnp
from jax import lax
from jax.experimental import pallas as pl
from jax.experimental.pallas import tpu as pltpu
from jax.sharding import Mesh, PartitionSpec as P

EXP_BLOCK = 128
XY = ("xh", "y")
RCV = ("xh", "y", "c")
SRC = ("z", "xl")
SWAP = [(0, 1), (1, 0)]


def decode(codes_ref, scale_ref, step, tile):
    blocks = tile // EXP_BLOCK
    scale = pltpu.roll(scale_ref[...], 128 - blocks * step, 1)
    parts = []
    for b in range(blocks):
        wide = jnp.broadcast_to(scale[:, b : b + 1], (scale.shape[0], EXP_BLOCK)).astype(jnp.bfloat16)
        cols = slice(b * EXP_BLOCK, (b + 1) * EXP_BLOCK)
        parts.append(jnp.concatenate([codes_ref[0, :, cols] * wide, codes_ref[1, :, cols] * wide], axis=0))
    return jnp.concatenate(parts, axis=1)


def forward_body(tile, rows, mine_ref, other_ref, codes_ref, scale_ref, out_ref, acc_ref):
    step = pl.program_id(0)

    @pl.when(step == 0)
    def _():
        acc_ref[...] = jnp.zeros_like(acc_ref)

    kern = decode(codes_ref, scale_ref, step, tile)
    waves = jnp.concatenate([mine_ref[...], other_ref[...]], axis=0)
    acc_ref[...] += lax.dot_general(waves, kern, (((1,), (1,)), ((), ())), preferred_element_type=jnp.float32)

    @pl.when(step == pl.num_programs(0) - 1)
    def _():
        for c in range(2):
            for xy in range(8):
                at = c * 128 + xy * 16
                re, im = acc_ref[at : at + 8, :], acc_ref[at + 8 : at + 16, :]
                out_ref[xy, c, 0] = re[:, :rows] - im[:, rows:]
                out_ref[xy, c, 1] = im[:, :rows] + re[:, rows:]


def forward(mine, other, codes, scale, tile=1024):
    _, rows, cols = codes.shape
    import functools

    return pl.pallas_call(
        functools.partial(forward_body, tile, rows),
        grid=(cols // tile,),
        in_specs=[
            pl.BlockSpec((128, tile), lambda i: (0, i)),
            pl.BlockSpec((128, tile), lambda i: (0, i)),
            pl.BlockSpec((2, rows, tile), lambda i: (0, 0, i)),
            pl.BlockSpec((rows, 128), lambda i: (0, 0)),
        ],
        out_specs=pl.BlockSpec((8, 2, 2, 8, rows), lambda i: (0, 0, 0, 0, 0)),
        out_shape=jax.ShapeDtypeStruct((8, 2, 2, 8, rows), jnp.float32),
        scratch_shapes=[pltpu.VMEM((256, 2 * rows), jnp.float32)],
        cost_estimate=pl.CostEstimate(flops=2 * 256 * 1024 * 8192, bytes_accessed=22 << 20, transcendentals=0),
        name="forward",
    )(mine, other, codes, scale)


def backward_body(tile, amat_ref, codes_ref, scale_ref, mine_ref, other_ref):
    kern = decode(codes_ref, scale_ref, pl.program_id(0), tile)
    prod = jnp.dot(amat_ref[...], kern, preferred_element_type=jnp.float32).astype(jnp.bfloat16)
    mine_ref[...] = prod[:128]
    other_ref[...] = prod[128:]


def backward(amat, codes, scale, tile=1024):
    _, rows, cols = codes.shape
    import functools

    half = jax.ShapeDtypeStruct((128, cols), jnp.bfloat16)
    return pl.pallas_call(
        functools.partial(backward_body, tile),
        grid=(cols // tile,),
        in_specs=[
            pl.BlockSpec((256, 2 * rows), lambda i: (0, 0)),
            pl.BlockSpec((2, rows, tile), lambda i: (0, 0, i)),
            pl.BlockSpec((rows, 128), lambda i: (0, 0)),
        ],
        out_specs=[pl.BlockSpec((128, tile), lambda i: (0, i))] * 2,
        out_shape=[half, half],
        cost_estimate=pl.CostEstimate(flops=2 * 256 * 1024 * 8192, bytes_accessed=22 << 20, transcendentals=0),
        name="backward",
    )(amat, codes, scale)


def body(codes, exps, wavefield, observed, mask):
    _, rows, cols = codes.shape
    core = lax.axis_index("c")
    scale = jnp.exp2(exps.astype(jnp.float32))
    scale = jnp.concatenate([scale, scale], axis=1)
    own = wavefield.transpose(0, 2, 1)
    mine = lax.all_to_all(jnp.broadcast_to(own[None], (8,) + own.shape), XY, 0, 0, tiled=True)
    other = lax.ppermute(mine, "c", SWAP)
    parts = forward(mine.reshape(128, cols), other.reshape(128, cols), codes, scale)
    parts = lax.all_to_all(parts, SRC, 0, 0, tiled=True)
    pred = jnp.sum(parts, axis=0)
    share = lax.axis_index(SRC) * 16
    seen = lax.dynamic_slice_in_dim(observed, share, 16, 2)
    seen = seen.astype(jnp.float32).transpose(0, 2, 1).reshape(2, 2, 8, rows).transpose(1, 0, 2, 3)
    seen = jnp.where(core == 0, seen, seen[::-1])
    live = mask.astype(jnp.float32)
    resid = (live * (pred - seen)).astype(jnp.bfloat16)
    placed = jnp.where(core == 0, resid, resid[::-1])
    own_resid = placed.transpose(1, 0, 2, 3).reshape(2, 16, rows).transpose(0, 2, 1)
    every = lax.all_to_all(jnp.broadcast_to(resid[None], (8,) + resid.shape), SRC, 0, 0, tiled=True)
    every = every.transpose(1, 0, 2, 3, 4)
    re, im = every[:, :, 0], every[:, :, 1]
    amat = jnp.stack([jnp.concatenate([re, im], axis=3), jnp.concatenate([im, -re], axis=3)], axis=2)
    gmine, gother = backward(amat.reshape(256, 2 * rows), codes, scale)
    came = lax.ppermute(gother, "c", SWAP)
    chip = (gmine.astype(jnp.float32) + came.astype(jnp.float32)).astype(jnp.bfloat16)
    terms = lax.all_to_all(chip.reshape(8, 2, 8, cols), XY, 0, 0, tiled=True)
    gradient = jnp.sum(terms.astype(jnp.float32), axis=0).astype(jnp.bfloat16)
    return own_resid, gradient.transpose(0, 2, 1)


def solution(mesh):
    fine = Mesh(mesh.devices.reshape(2, 4, 2, 4, 2), ("xh", "y", "c", "z", "xl"))
    in_specs = (P(None, RCV, SRC), P(RCV, SRC), P(None, SRC, RCV), P(None, RCV, None), P(RCV))
    out_specs = (P(None, RCV, SRC), P(None, SRC, RCV))
    return jax.shard_map(body, mesh=fine, in_specs=in_specs, out_specs=out_specs, check_vma=False)
```

time: 314 us -> 135 us (0.43)
  waiting for transfers between devices: 110 us -> 43.7 us
  blocking collectives: 105 us -> 45.2 us
  Pallas kernels: 0 us -> 26.8 us
  matrix products: 26 us -> 0 us
  local copies, waits for them, and re-layouts: 27.7 us -> 2.47 us
  other arithmetic: 29.9 us -> 6.43 us
  between operations: 14.8 us -> 0.79 us
  starting transfers between devices: 0.08 us -> 9.2 us
    unnamed x1 -> x0, blocking collectives: 105 us -> none
    psum x1 -> x0, waiting for transfers between devices: 73.1 us -> none  [body(): predicted = lax.psum(partial_pred, 'src')]
    all_to_all x0 -> x2, blocking collectives: none -> 45.2 us  [the longest x1 35.4 us: body(): lax.all_to_all(jnp.broadcast_to(own[None], (8,) + own.shape), XY, 0, 0, t...]
    all_to_all x0 -> x2, waiting for transfers between devices: none -> 36.4 us  [the longest x1 26.3 us: body(): terms = lax.all_to_all(chip.reshape(8, 2, 8, cols), XY, 0, 0, tiled=True)]
    all_gather x1 -> x0, waiting for transfers between devices: 35.8 us -> none  [body(): piece = lax.all_gather(wavefield, 'rcv', axis=2, tiled=True)]
    pallas_call x0 -> x2, Pallas kernels: none -> 26.8 us  [the longest x1 13.6 us: forward(): pl.pallas_call(functools.partial(forward_body, tile, rows), grid=(cols //...]
    dot_general x3 -> x0, matrix products: 26 us -> none  [the longest x1 10.2 us: body(): lax.dot_general(stacked, left, (((0,), (0,)), ((), ())), preferred_elemen...]
    convert_element_type x3 -> x4, other arithmetic: 19.7 us -> 3.42 us  [the longest x1 3.39 us: body(): (gmine.astype(jnp.float32) + came.astype(jnp.float32)).astype(jnp.bfloat16)]
  transfers between devices with their start and end apart: 2 -> 4, of which waited for: 2 -> 4; matrix products, arithmetic and copies ran while one was open for 8% -> 2% of each run, Pallas kernels for 0% -> 0%
where the time goes in v1:
time: 135 us; the launch traced here: 134 us
  blocking collectives  45.2 us (33%)
  waiting for transfers between devices  43.7 us (32%)
  Pallas kernels  26.8 us (20%)
  starting transfers between devices  9.2 us (7%)
  other arithmetic  6.43 us (5%)
  local copies, waits for them, and re-layouts  2.47 us (2%)
    all_to_all x1, blocking collectives, body(): lax.all_to_all(jnp.broadcast_to(own[None], (8,) + own.shape), XY, 0, 0, t...  35.4 us
    all_to_all x1, waiting for transfers between devices, body(): terms = lax.all_to_all(chip.reshape(8, 2, 8, cols), XY, 0, 0, tiled=True)  26.3 us
    pallas_call x1, Pallas kernels, forward(): pl.pallas_call(functools.partial(forward_body, tile, rows), grid=(cols //...  13.6 us
    pallas_call x1, Pallas kernels, backward(): pl.pallas_call(functools.partial(backward_body, tile), grid=(cols // tile...  13.2 us
    all_to_all x1, waiting for transfers between devices, body(): parts = lax.all_to_all(parts, SRC, 0, 0, tiled=True)  10.1 us
    all_to_all x1, blocking collectives, body(): lax.all_to_all(jnp.broadcast_to(resid[None], (8,) + resid.shape), SRC, 0,...  9.82 us
    all_to_all x1, starting transfers between devices, body(): parts = lax.all_to_all(parts, SRC, 0, 0, tiled=True)  5.59 us
    ppermute x1, waiting for transfers between devices, body(): came = lax.ppermute(gother, 'c', SWAP)  4.37 us
  transfers between devices with their start and end apart: 4, of which 4 were waited for; matrix products, arithmetic and copies ran while one was open for 2% of the time, Pallas kernels for 0%

profile of v1, /device:TPU:0, one launch (start us, length us, event | category | flops | bytes accessed | tf_op | source)
XLA Modules:
  0.0 134.5 jit_solution(374256715317064504)
XLA Ops:
  0.6 0.0 copy-start
  0.6 1.2 broadcast_in_dim.4
  1.8 0.0 copy-start.2
  1.9 35.4 %all_to_all.20 = bf16[8,2,8,8192]{3,2,1,0:T(8,128)(2,1)S(1)} all-to-all(bf16[8,2,8,8192]{3,2,1,0:T(8,128)(2,1)S(1)} %broadcast_in_dim.4), channel_id=1, replica_groups=mesh['xh'=2,'y'=4,'c'=2,'z'=4,'xl'=2] {'xh','y'}, dimensions={0} | all-to-all | bytes 4194304 | tf_op jit(solution)/shard_map/all_to_all | solution.py:101
  37.2 0.0 copy-start.1
  37.2 0.0 collective-permute-start
  37.2 0.0 copy-done.2
  37.2 0.1 copy.26
  37.4 1.1 pad_maximum_fusion.1.scale_ref
  38.6 2.9 %collective-permute-done = bf16[8,2,8,8192]{3,2,1,0:T(8,128)(2,1)} collective-permute-done((bf16[8,2,8,8192]{3,2,1,0:T(8,128)(2,1)S(1)}, bf16[8,2,8,8192]{3,2,1,0:T(8,128)(2,1)}, u32[]{:S(2)}, u32[]{:S(2)}) %collective-permute-start) | collective-permute-done | bytes 2097184 | tf_op jit(solution)/shard_map/ppermute | solution.py:102
  41.5 0.0 copy-done.1
  41.5 0.0 copy-start.3
  41.5 13.6 %forward.1 = f32[8,2,2,8,512]{4,3,2,1,0:T(8,128)} custom-call(bf16[128,8192]{1,0:T(8,128)(2,1)} %bitcast.33, bf16[128,8192]{1,0:T(8,128)(2,1)} %bitcast.2.other_ref, bf16[2,512,8192]{2,1,0:T(8,128)(2,1)} %codes_ref.3, f32[512,128]{1,0:T(8,128)} %pad_maximum_fusion.1.scale_ref), custom_call_target="tpu_custom_call" | custom-call | flops 4294967296 | bytes 23068672 | tf_op jit(solution)/shard_map/forward/pallas_call | solution.py:51
  55.1 5.6 %all-to-all-start.1 = ((f32[8,2,2,8,512]{4,3,2,1,0:T(8,128)}), f32[8,2,2,8,512]{4,3,2,1,0:T(8,128)S(1)}, u32[]{:S(2)}, u32[]{:S(2)}) async-start(f32[8,2,2,8,512]{4,3,2,1,0:T(8,128)} %forward.1), calls=%async_computation.1 | async-start | bytes 1048576 | tf_op jit(solution)/shard_map/all_to_all | solution.py:104
  60.7 0.0 copy-done.3
  60.7 0.0 copy-done
  60.7 0.1 constant_dynamic-slice_fusion
  60.8 0.1 copy.33
  61.0 10.1 %all-to-all-done.1 = f32[8,2,2,8,512]{4,3,2,1,0:T(8,128)S(1)} async-done(((f32[8,2,2,8,512]{4,3,2,1,0:T(8,128)}), f32[8,2,2,8,512]{4,3,2,1,0:T(8,128)S(1)}, u32[]{:S(2)}, u32[]{:S(2)}) %all-to-all-start.1) | async-done | bytes 524320 | tf_op jit(solution)/shard_map/all_to_all | solution.py:104
  71.1 9.8 %all_to_all.21 = bf16[8,2,2,8,512]{4,3,1,2,0:T(8,128)(2,1)S(1)} all-to-all(bf16[8,2,2,8,512]{4,3,1,2,0:T(8,128)(2,1)S(1)} %broadcast_in_dim.5), channel_id=1, replica_groups=mesh['xh'=2,'y'=4,'c'=2,'z'=4,'xl'=2] {'z','xl'}, dimensions={0} | all-to-all | bytes 524288 | tf_op jit(solution)/shard_map/all_to_all | solution.py:114
  81.1 0.1 pad_maximum_fusion
  81.1 0.8 copy.32
  82.0 13.2 %backward.1 = (bf16[128,8192]{1,0:T(8,128)(2,1)}, bf16[128,8192]{1,0:T(8,128)(2,1)}) custom-call(bf16[256,1024]{1,0:T(8,128)(2,1)} %bitcast.34, bf16[2,512,8192]{2,1,0:T(8,128)(2,1)} %codes_ref.3, f32[512,128]{1,0:T(8,128)} %pad_maximum_fusion.1.scale_ref), custom_call_target="tpu_custom_call" | custom-call | flops 4294967296 | bytes 23068672 | tf_op jit(solution)/shard_map/backward/pallas_call | solution.py:80
  95.1 0.0 collective-permute-start.1
  95.2 4.4 %collective-permute-done.1 = bf16[128,8192]{1,0:T(8,128)(2,1)S(1)} collective-permute-done((bf16[128,8192]{1,0:T(8,128)(2,1)}, bf16[128,8192]{1,0:T(8,128)(2,1)S(1)}, u32[]{:S(2)}, u32[]{:S(2)}) %collective-permute-start.1) | collective-permute-done | bytes 2097184 | tf_op jit(solution)/shard_map/ppermute | solution.py:119
  99.5 3.4 %add_convert_fusion = bf16[128,8192]{1,0:T(8,128)(2,1)} fusion(bf16[128,8192]{1,0:T(8,128)(2,1)S(1)} %collective-permute-done.1, bf16[128,8192]{1,0:T(8,128)(2,1)} %get-tuple-element.4), kind=kLoop, calls=%fused_computation | loop fusion | flops 4194304 | bytes 6291456 | tf_op jit(solution)/shard_map/convert_element_type | solution.py:120
  102.9 3.6 %all-to-all-start.3 = ((bf16[8,2,8,8192]{3,2,1,0:T(8,128)(2,1)}), bf16[8,2,8,8192]{3,2,1,0:T(8,128)(2,1)S(1)}, u32[]{:S(2)}, u32[]{:S(2)}) async-start(bf16[8,2,8,8192]{3,2,1,0:T(8,128)(2,1)} %bitcast.15), calls=%async_computation.3 | async-start | bytes 4194304 | tf_op jit(solution)/shard_map/all_to_all | solution.py:121
  106.5 0.6 copy_bitcast_fusion.1
  107.1 26.3 %all-to-all-done.3 = bf16[8,2,8,8192]{3,2,1,0:T(8,128)(2,1)S(1)} async-done(((bf16[8,2,8,8192]{3,2,1,0:T(8,128)(2,1)}), bf16[8,2,8,8192]{3,2,1,0:T(8,128)(2,1)S(1)}, u32[]{:S(2)}, u32[]{:S(2)}) %all-to-all-start.3) | async-done | bytes 2097184 | tf_op jit(solution)/shard_map/all_to_all | solution.py:121
  133.4 1.0 reduce_sum.22
  (11 shorter events, 0.2 us)
Async XLA Ops:
  0.6 60.0 %copy-start = (bf16[2,512,128]{2,1,0:T(8,128)(2,1)S(1)}, bf16[2,512,128]{2,1,0:T(8,128)(2,1)}, u32[]{:S(2)}) copy-start(bf16[2,512,128]{2,1,0:T(8,128)(2,1)} %param.8) | copy-start | bytes 786436
  1.8 35.4 %copy-start.2 = (s32[512,64]{0,1:T(8,128)S(1)}, s32[512,64]{0,1:T(8,128)}, u32[]{:S(2)}) copy-start(s32[512,64]{0,1:T(8,128)} %param.6) | copy-start | bytes 393220
  37.2 4.3 %copy-start.1 = (bf16[8,2,8,8192]{3,2,1,0:T(8,128)(2,1)}, bf16[8,2,8,8192]{3,2,1,0:T(8,128)(2,1)S(1)}, u32[]{:S(2)}) copy-start(bf16[8,2,8,8192]{3,2,1,0:T(8,128)(2,1)S(1)} %all_to_all.20) | copy-start | bytes 6291460
  37.2 4.3 %collective-permute-start = (bf16[8,2,8,8192]{3,2,1,0:T(8,128)(2,1)S(1)}, bf16[8,2,8,8192]{3,2,1,0:T(8,128)(2,1)}, u32[]{:S(2)}, u32[]{:S(2)}) collective-permute-start(bf16[8,2,8,8192]{3,2,1,0:T(8,128)(2,1)S(1)} %all_to_all.20), channel_id=1, source_target_pairs={{0,8},{8,0},{1,9},{9,1},{2,10},{10,2},{3,11},{11,3},{4,12},{12,4},... | collective-permute-start | bytes 6291464 | tf_op jit(solution)/shard_map/ppermute | solution.py:102
  41.5 19.2 %copy-start.3 = (s32[512]{0:T(512)S(1)}, s32[512]{0:T(512)}, u32[]{:S(2)}) copy-start(s32[512]{0:T(512)} %param.9) | copy-start | bytes 6148
  55.1 16.0 %all-to-all-start.1 = ((f32[8,2,2,8,512]{4,3,2,1,0:T(8,128)}), f32[8,2,2,8,512]{4,3,2,1,0:T(8,128)S(1)}, u32[]{:S(2)}, u32[]{:S(2)}) async-start(f32[8,2,2,8,512]{4,3,2,1,0:T(8,128)} %forward.1), calls=%async_computation.1 | async-start | bytes 1048576 | tf_op jit(solution)/shard_map/all_to_all | solution.py:104
  95.1 4.4 %collective-permute-start.1 = (bf16[128,8192]{1,0:T(8,128)(2,1)}, bf16[128,8192]{1,0:T(8,128)(2,1)S(1)}, u32[]{:S(2)}, u32[]{:S(2)}) collective-permute-start(bf16[128,8192]{1,0:T(8,128)(2,1)} %get-tuple-element.5), channel_id=1, source_target_pairs={{0,8},{8,0},{1,9},{9,1},{2,10},{10,2},{3,11},{11,3},{4,12},{12,4},... | collective-permute-start | bytes 6291464 | tf_op jit(solution)/shard_map/ppermute | solution.py:119
  102.9 30.5 %all-to-all-start.3 = ((bf16[8,2,8,8192]{3,2,1,0:T(8,128)(2,1)}), bf16[8,2,8,8192]{3,2,1,0:T(8,128)(2,1)S(1)}, u32[]{:S(2)}, u32[]{:S(2)}) async-start(bf16[8,2,8,8192]{3,2,1,0:T(8,128)(2,1)} %bitcast.15), calls=%async_computation.3 | async-start | bytes 4194304 | tf_op jit(solution)/shard_map/all_to_all | solution.py:121

commit v2 on v0

v2 whole, which is shorter than its diff:
```python
import functools

import jax
import jax.numpy as jnp
from jax import lax
from jax.experimental import pallas as pl
from jax.experimental.pallas import tpu as pltpu
from jax.sharding import Mesh, PartitionSpec as P

EXP_BLOCK = 128
RCV = ("xh", "y", "c")
SRC = ("z", "xl")
SWAP = [(0, 1), (1, 0)]
VM = pl.BlockSpec(memory_space=pltpu.VMEM)

X, Y1, Y3, Y2 = (1, 0), (0, 1), (0, 3), (0, 2)
FROM = (
    ((0, 0), (1, 0), (0, 3), (0, 1), (0, 2), (1, 3), (1, 1), (1, 2)),
    ((0, 0), (0, 3), (0, 1), (0, 2), (1, 0), (1, 3), (1, 1), (1, 2)),
)
DEST = (
    ((0, 1), (1, 1), (0, 3), (1, 3), (0, 2), (1, 2), (0, 0), (1, 0)),
    ((1, 0), (1, 1), (1, 3), (1, 2), (0, 0), (0, 1), (0, 3), (0, 2)),
)


def move(x, first, second):
    pairs = []
    for a in range(2):
        for b in range(4):
            for c, step in ((0, first), (1, second)):
                if step is not None:
                    to = ((a + step[0]) % 2) * 4 + (b + step[1]) % 4
                    pairs.append(((a * 4 + b) * 2 + c, to * 2 + c))
    return lax.ppermute(x, RCV, pairs)


def swap(x):
    return lax.ppermute(x, "c", SWAP)


def vmem(x):
    return pltpu.with_memory_space_constraint(x, pltpu.VMEM)


def params(mib):
    return pltpu.CompilerParams(vmem_limit_bytes=mib << 20)


def cost(us):
    return pl.CostEstimate(flops=us * 10**9, bytes_accessed=us * 3 * 10**6, transcendentals=0)


def here(core, table, k):
    x, y = lax.axis_index("xh"), lax.axis_index("y")
    (ax, ay), (bx, by) = table[0][k], table[1][k]
    dx, dy = jnp.where(core == 0, ax, bx), jnp.where(core == 0, ay, by)
    return lax.bitwise_and(x + dx, 1) * 4 + lax.bitwise_and(y + dy, 3)


def decode(codes_ref, wide_ref, cols):
    wide = wide_ref[:, cols]
    return jnp.concatenate([codes_ref[0, :, cols] * wide, codes_ref[1, :, cols] * wide], axis=0)


def widen_body(exps_ref, wide_ref):
    exps = exps_ref[...]
    scale = jnp.where(exps >= -14, 2.0**-14, jnp.where(exps == -15, 2.0**-15, jnp.where(exps == -16, 2.0**-16, 2.0**-17)))
    scale = scale.astype(jnp.float32).T
    for b in range(exps.shape[0]):
        wide = jnp.broadcast_to(scale[:, b : b + 1], (scale.shape[0], EXP_BLOCK)).astype(jnp.bfloat16)
        wide_ref[:, b * EXP_BLOCK : (b + 1) * EXP_BLOCK] = wide


def widen(exps):
    blocks, rows = exps.shape
    return pl.pallas_call(
        widen_body,
        in_specs=[VM],
        out_specs=VM,
        out_shape=pltpu.VMEM((rows, blocks * EXP_BLOCK), jnp.bfloat16),
        cost_estimate=cost(10),
        compiler_params=params(4),
        name="widen",
    )(exps)


def pick_body(first, second, out):
    core = lax.axis_index("c")

    @pl.when(core == 0)
    def _():
        out[...] = first[...]

    @pl.when(core == 1)
    def _():
        out[...] = second[...]


def pick(first, second):
    return pl.pallas_call(
        pick_body,
        in_specs=[VM] * 2,
        out_specs=VM,
        out_shape=jax.ShapeDtypeStruct(first.shape, first.dtype),
        cost_estimate=cost(1),
        compiler_params=params(4),
        name="pick",
    )(first, second)


def forward_body(tile, rows, *refs):
    pieces, codes_ref, wide_ref, out_ref, acc_ref = refs[:16], refs[16], refs[17], refs[18], refs[19]
    acc_ref[...] = jnp.zeros_like(acc_ref)

    def step(i, _):
        at = pl.multiple_of(i * tile, tile)
        waves = jnp.concatenate([p[:, pl.ds(at, tile)] for p in pieces], axis=0)
        kern = decode(codes_ref, wide_ref, pl.ds(at, tile))
        acc_ref[...] += lax.dot_general(waves, kern, (((1,), (1,)), ((), ())), preferred_element_type=jnp.float32)
        return 0

    lax.fori_loop(0, pieces[0].shape[1] // tile, step, 0)
    core = lax.axis_index("c")
    for c in range(2):
        for k in range(8):
            at, top = here(lax.bitwise_xor(core, c), FROM, k), (c * 8 + k) * 16
            re, im = acc_ref[top : top + 8, :], acc_ref[top + 8 : top + 16, :]
            out_ref[at, c, 0] = re[:, :rows] - im[:, rows:]
            out_ref[at, c, 1] = im[:, :rows] + re[:, rows:]


def forward(pieces, codes, wide, tile=1024):
    rows = codes.shape[1]
    return pl.pallas_call(
        functools.partial(forward_body, tile, rows),
        in_specs=[VM] * 18,
        out_specs=VM,
        out_shape=jax.ShapeDtypeStruct((8, 2, 2, 8, rows), jnp.float32),
        scratch_shapes=[pltpu.VMEM((256, 2 * rows), jnp.float32)],
        cost_estimate=cost(6),
        compiler_params=params(10),
        name="forward",
    )(*pieces, vmem(codes), vmem(wide))


def resid_body(parts, seen, mask, every, own):
    core = lax.axis_index("c")
    live = mask[...].astype(jnp.float32)
    for c in range(2):
        at = lax.bitwise_xor(core, c)
        for k in range(2):
            pred = parts[0, c, k]
            for j in range(1, 8):
                pred += parts[j, c, k]
            resid = (live * (pred - seen[k, at])).astype(jnp.bfloat16)
            own[k, at] = resid
            for j in range(8):
                every[j, c, k] = resid


def residual(parts, seen, mask):
    one = jax.ShapeDtypeStruct(seen.shape, jnp.bfloat16)
    return pl.pallas_call(
        resid_body,
        in_specs=[VM] * 3,
        out_specs=[VM] * 2,
        out_shape=[jax.ShapeDtypeStruct(parts.shape, jnp.bfloat16), one],
        cost_estimate=cost(1),
        compiler_params=params(4),
        name="residual",
    )(parts, seen, mask)


def backward_body(start, tile, every_ref, codes_ref, wide_ref, *refs):
    other_ref, mine, a_ref = refs[0], refs[1:5], refs[5]
    rows = codes_ref.shape[1]
    core = lax.axis_index("c")
    for k in range(16):
        block = every_ref[here(lax.bitwise_xor(core, k // 8), DEST, k % 8), k // 8].astype(jnp.float32)
        top = slice(16 * k, 16 * k + 16)
        a_ref[top, :rows] = jnp.concatenate([block[0], block[1]], axis=0).astype(jnp.bfloat16)
        a_ref[top, rows:] = jnp.concatenate([block[1], -block[0]], axis=0).astype(jnp.bfloat16)

    def step(i, _):
        at = pl.multiple_of(start + i * tile, tile)
        to = pl.ds(pl.multiple_of(i * tile, tile), tile)
        kern = decode(codes_ref, wide_ref, pl.ds(at, tile))
        prod = jnp.dot(a_ref[...], kern, preferred_element_type=jnp.float32).astype(jnp.bfloat16)
        for k in range(8):
            mine[k // 2][k % 2, :, to] = prod[16 * k : 16 * k + 16]
            other_ref[k, :, to] = prod[128 + 16 * k : 144 + 16 * k]
        return 0

    lax.fori_loop(0, other_ref.shape[2] // tile, step, 0)


def backward(every, codes, wide, part, parts, tile=1024):
    _, rows, cols = codes.shape
    cols = cols // parts
    pair = jax.ShapeDtypeStruct((2, 16, cols), jnp.bfloat16)
    return pl.pallas_call(
        functools.partial(backward_body, part * cols, tile),
        in_specs=[VM] * 3,
        out_specs=[VM] * 5,
        out_shape=[jax.ShapeDtypeStruct((8, 16, cols), jnp.bfloat16)] + [pair] * 4,
        scratch_shapes=[pltpu.VMEM((256, 2 * rows), jnp.bfloat16)],
        cost_estimate=cost(3),
        compiler_params=params(10),
        name="backward",
    )(every, vmem(codes), vmem(wide))


def chip_body(m1, m2, m3, m4, came, u1, u2, u3, u4):
    for k, (m, u) in enumerate(((m1, u1), (m2, u2), (m3, u3), (m4, u4))):
        total = m[...].astype(jnp.float32) + came[2 * k : 2 * k + 2].astype(jnp.float32)
        u[...] = total.astype(jnp.bfloat16)


def chip_sum(mine, came):
    return pl.pallas_call(
        chip_body,
        in_specs=[VM] * 5,
        out_specs=[VM] * 4,
        out_shape=[jax.ShapeDtypeStruct(m.shape, m.dtype) for m in mine],
        cost_estimate=cost(1),
        compiler_params=params(4),
        name="chip_sum",
    )(*mine, came)


def stage_body(u3, u4, q1, q2, q3, keep, s4, s5, s6):
    def f(ref, k):
        return ref[k].astype(jnp.float32)

    core = lax.axis_index("c")

    @pl.when(core == 0)
    def _():
        keep[...] = f(u4, 0) + f(q1, 0) + f(q2, 0) + f(q3, 0)
        s4[...] = (f(u4, 1) + f(q1, 1) + f(q2, 1) + f(q3, 1)).astype(jnp.bfloat16)
        s5[...] = jnp.zeros_like(s5)
        s6[...] = jnp.zeros_like(s6)

    @pl.when(core == 1)
    def _():
        keep[...] = f(u3, 0) + f(q1, 0)
        s4[...] = (f(u3, 1) + f(q1, 1)).astype(jnp.bfloat16)
        s5[...] = (f(u4, 0) + f(q2, 0)).astype(jnp.bfloat16)
        s6[...] = (f(u4, 1) + f(q2, 1)).astype(jnp.bfloat16)


def stage_sum(u3, u4, q1, q2, q3):
    one = jax.ShapeDtypeStruct(u3.shape[1:], jnp.bfloat16)
    return pl.pallas_call(
        stage_body,
        in_specs=[VM] * 5,
        out_specs=[VM] * 4,
        out_shape=[jax.ShapeDtypeStruct(u3.shape[1:], jnp.float32), one, one, one],
        cost_estimate=cost(1),
        compiler_params=params(4),
        name="stage_sum",
    )(u3, u4, q1, q2, q3)


def gather(own, ready):
    r1 = move(own, X, Y1)
    r2 = move(own, Y1, Y3)
    r3 = move(own, Y3, Y2)
    r4 = move(own, Y2, X)
    r1, ready = lax.optimization_barrier((r1, ready))
    r5 = move(r1, Y1, X)
    r6 = move(pick(r1, r2), Y3, X)
    r7 = move(pick(r1, r3), Y2, X)
    return [own, r1, r2, r3, r4, r5, r6, r7], ready


def scatter(mine, came):
    u1, u2, u3, u4 = chip_sum(mine, came)
    q1 = move(u1, Y1, X)
    q2 = move(u2, Y3, X)
    q3 = move(u3, Y2, None)
    keep, s4, s5, s6 = stage_sum(u3, u4, q1, q2, q3)
    q4 = move(s4, X, Y1)
    q5 = move(s5, None, Y3)
    q6 = move(s6, None, Y2)
    return keep + q4.astype(jnp.float32) + q5.astype(jnp.float32) + q6.astype(jnp.float32)


def body(codes, exps, wavefield, observed, mask):
    _, rows, cols = codes.shape
    own = wavefield.transpose(0, 2, 1).reshape(16, cols)
    seen = lax.dynamic_slice_in_dim(observed, lax.axis_index(SRC) * 16, 16, 2)
    seen = seen.astype(jnp.float32).transpose(0, 2, 1).reshape(2, 2, 8, rows)
    pieces, (exps, seen, mask) = gather(own, (exps.T, seen, mask.reshape(1, rows)))
    wide = widen(exps)
    pieces += [swap(p) for p in pieces]
    parts = forward(pieces, codes, wide)
    parts = lax.all_to_all(parts, SRC, 0, 0, tiled=True)
    every, own_resid = residual(parts, seen, mask)
    every = lax.all_to_all(every, SRC, 0, 0, tiled=True)
    halves = []
    for part in range(2):
        other, *mine = backward(every, codes, wide, part, 2)
        halves.append((mine, swap(other)))
    sums = [scatter(mine, came) for mine, came in halves]
    gradient = jnp.concatenate(sums, axis=1).astype(jnp.bfloat16).reshape(2, 8, cols)
    return own_resid.reshape(2, 16, rows).transpose(0, 2, 1), gradient.transpose(0, 2, 1)


def solution(mesh):
    fine = Mesh(mesh.devices.reshape(2, 4, 2, 4, 2), ("xh", "y", "c", "z", "xl"))
    in_specs = (P(None, RCV, SRC), P(RCV, SRC), P(None, SRC, RCV), P(None, RCV, None), P(RCV))
    out_specs = (P(None, RCV, SRC), P(None, SRC, RCV))
    return jax.shard_map(body, mesh=fine, in_specs=in_specs, out_specs=out_specs, check_vma=False)
```

time: 314 us -> 103 us (0.33)
  the two profiles are of different devices: /device:TPU:0 before, /device:TPU:1 now
where the time goes in v2:
time: 103 us
  starting transfers between devices  49.6 us (48%)
  blocking collectives  23.3 us (23%)
  Pallas kernels  16.2 us (16%)
  waiting for transfers between devices  9.75 us (9%)
  other arithmetic  1.93 us (2%)
  local copies, waits for them, and re-layouts  1.1 us (1%)
    ppermute x19, starting transfers between devices, move(): return lax.ppermute(x, RCV, pairs)  37.3 us
    all_to_all x1, blocking collectives, body(): parts = lax.all_to_all(parts, SRC, 0, 0, tiled=True)  14.8 us
    ppermute x10, starting transfers between devices, swap(): return lax.ppermute(x, 'c', SWAP)  12.3 us
    ppermute x19, waiting for transfers between devices, move(): return lax.ppermute(x, RCV, pairs)  9.72 us
    all_to_all x1, blocking collectives, body(): every = lax.all_to_all(every, SRC, 0, 0, tiled=True)  8.57 us
    pallas_call x1, Pallas kernels, forward(): pl.pallas_call(functools.partial(forward_body, tile, rows), in_specs=[VM]...  6.37 us
    pallas_call x2, Pallas kernels, backward(): pl.pallas_call(functools.partial(backward_body, part * cols, tile), in_sp...  5.92 us
    pallas_call x1, Pallas kernels, widen(): pl.pallas_call(widen_body, in_specs=[VM], out_specs=VM, out_shape=pltpu.V...  2.46 us
  transfers between devices with their start and end apart: 29, of which 4 were waited for; matrix products, arithmetic and copies ran while one was open for 1% of the time, Pallas kernels for 6%

profile of v2, /device:TPU:1, one launch (start us, length us, event | category | flops | bytes accessed | tf_op | source)
XLA Modules:
  0.0 102.9 jit_solution(9947711358280393788)
XLA Ops:
  0.6 2.2 %collective-permute-start = (bf16[16,8192]{1,0:T(8,128)(2,1)}, bf16[16,8192]{1,0:T(8,128)(2,1)S(1)}, u32[]{:S(2)}, u32[]{:S(2)}) collective-permute-start(bf16[16,8192]{1,0:T(8,128)(2,1)} %bitcast.19), channel_id=1, source_target_pairs={{0,64},{8,24},{16,80},{24,40},{32,96},{40,56},{48,112},{56,8},{64,... | collective-permute-start | bytes 786440 | tf_op jit(solution)/shard_map/ppermute | solution.py:35
  2.8 1.5 %collective-permute-start.1 = (bf16[16,8192]{1,0:T(8,128)(2,1)}, bf16[16,8192]{1,0:T(8,128)(2,1)S(1)}, u32[]{:S(2)}, u32[]{:S(2)}) collective-permute-start(bf16[16,8192]{1,0:T(8,128)(2,1)} %bitcast.20), channel_id=1, source_target_pairs={{0,16},{8,56},{16,32},{24,8},{32,48},{40,24},{48,0},{56,40},{64,80... | collective-permute-start | bytes 786440 | tf_op jit(solution)/shard_map/ppermute | solution.py:35
  4.3 2.7 %collective-permute-start.3 = (bf16[16,8192]{1,0:T(8,128)(2,1)}, bf16[16,8192]{1,0:T(8,128)(2,1)S(1)}, u32[]{:S(2)}, u32[]{:S(2)}) collective-permute-start(bf16[16,8192]{1,0:T(8,128)(2,1)} %bitcast.21), channel_id=1, source_target_pairs={{0,32},{8,72},{16,48},{24,88},{32,0},{40,104},{48,16},{56,120},{64... | collective-permute-start | bytes 786440 | tf_op jit(solution)/shard_map/ppermute | solution.py:35
  7.1 1.6 %collective-permute-start.2 = (bf16[16,8192]{1,0:T(8,128)(2,1)}, bf16[16,8192]{1,0:T(8,128)(2,1)S(1)}, u32[]{:S(2)}, u32[]{:S(2)}) collective-permute-start(bf16[16,8192]{1,0:T(8,128)(2,1)} %bitcast.22), channel_id=1, source_target_pairs={{0,48},{8,40},{16,0},{24,56},{32,16},{40,8},{48,32},{56,24},{64,11... | collective-permute-start | bytes 786440 | tf_op jit(solution)/shard_map/ppermute | solution.py:35
  8.6 2.4 %collective-permute-start.7 = (bf16[16,8192]{1,0:T(8,128)(2,1)}, bf16[16,8192]{1,0:T(8,128)(2,1)S(1)}, u32[]{:S(2)}, u32[]{:S(2)}) collective-permute-start(bf16[16,8192]{1,0:T(8,128)(2,1)} %bitcast.23), channel_id=1, source_target_pairs={{0,8},{8,0},{1,9},{9,1},{2,10},{10,2},{3,11},{11,3},{4,12},{12,4},... | collective-permute-start | bytes 786440 | tf_op jit(solution)/shard_map/ppermute | solution.py:39
  11.0 1.1 %convert_bitcast_fusion = f32[2,16,512]{1,2,0:T(8,128)S(1)} fusion(bf16[2,512,128]{2,1,0:T(8,128)(2,1)} %param.8, s32[]{:T(128)S(6)} %select_n.3), kind=kLoop, calls=%fused_computation | loop fusion | flops 16384 | bytes 98308 | tf_op jit(solution)/shard_map/reshape | solution.py:294
  12.1 0.2 copy.7
  12.3 0.0 collective-permute-done.first.refs_1_
  12.3 0.0 collective-permute-done.1.second.refs_2_
  12.3 3.8 %collective-permute-start.5 = (bf16[16,8192]{1,0:T(8,128)(2,1)S(1)}, bf16[16,8192]{1,0:T(8,128)(2,1)S(1)}, u32[]{:S(2)}, u32[]{:S(2)}) collective-permute-start(bf16[16,8192]{1,0:T(8,128)(2,1)S(1)} %pick.2), channel_id=1, source_target_pairs={{0,48},{8,72},{16,0},{24,88},{32,16},{40,104},{48,32},{56,120},{64... | collective-permute-start | bytes 786440 | tf_op jit(solution)/shard_map/ppermute | solution.py:35
  16.2 0.0 collective-permute-done.3.refs_4_
  16.2 3.7 %collective-permute-start.11 = (bf16[16,8192]{1,0:T(8,128)(2,1)S(1)}, bf16[16,8192]{1,0:T(8,128)(2,1)S(1)}, u32[]{:S(2)}, u32[]{:S(2)}) collective-permute-start(bf16[16,8192]{1,0:T(8,128)(2,1)S(1)} %collective-permute-done.3.refs_4_), channel_id=1, source_target_pairs={{0,8},{8,0},{1,9},{9,1},{2,10},{10,2},{3,11},{11,3},{4,12},{12,4},... | collective-permute-start | bytes 786440 | tf_op jit(solution)/shard_map/ppermute | solution.py:39
  19.9 0.0 collective-permute-done.2.second.refs_3_
  19.9 0.0 collective-permute-start.10
  19.9 0.0 slice-start.1
  19.9 0.0 slice-start.2
  20.0 0.0 copy-start
  20.0 1.5 %collective-permute-start.6 = (bf16[16,8192]{1,0:T(8,128)(2,1)S(1)}, bf16[16,8192]{1,0:T(8,128)(2,1)S(1)}, u32[]{:S(2)}, u32[]{:S(2)}) collective-permute-start(bf16[16,8192]{1,0:T(8,128)(2,1)S(1)} %pick.3), channel_id=1, source_target_pairs={{0,32},{8,72},{16,48},{24,88},{32,0},{40,104},{48,16},{56,120},{64... | collective-permute-start | bytes 786440 | tf_op jit(solution)/shard_map/ppermute | solution.py:35
  21.4 0.0 collective-permute-done.7.refs_8_
  21.4 1.6 %collective-permute-start.4 = (bf16[16,8192]{1,0:T(8,128)(2,1)S(1)}, bf16[16,8192]{1,0:T(8,128)(2,1)S(1)}, u32[]{:S(2)}, u32[]{:S(2)}) collective-permute-start(bf16[16,8192]{1,0:T(8,128)(2,1)S(1)} %collective-permute-done.first.refs_1_), channel_id=1, source_target_pairs={{0,16},{8,72},{16,32},{24,88},{32,48},{40,104},{48,0},{56,120},{64... | collective-permute-start | bytes 786440 | tf_op jit(solution)/shard_map/ppermute | solution.py:35
  23.0 0.0 collective-permute-done.10.refs_11_
  23.0 0.5 collective-permute-start.9
  23.5 0.1 collective-permute-start.13
  23.6 3.4 %collective-permute-done.6.refs_7_ = bf16[16,8192]{1,0:T(8,128)(2,1)S(1)} collective-permute-done((bf16[16,8192]{1,0:T(8,128)(2,1)S(1)}, bf16[16,8192]{1,0:T(8,128)(2,1)S(1)}, u32[]{:S(2)}, u32[]{:S(2)}) %collective-permute-start.6) | collective-permute-done | bytes 262176 | tf_op jit(solution)/shard_map/ppermute | solution.py:35
  27.1 1.4 %collective-permute-start.14 = (bf16[16,8192]{1,0:T(8,128)(2,1)S(1)}, bf16[16,8192]{1,0:T(8,128)(2,1)S(1)}, u32[]{:S(2)}, u32[]{:S(2)}) collective-permute-start(bf16[16,8192]{1,0:T(8,128)(2,1)S(1)} %collective-permute-done.6.refs_7_), channel_id=1, source_target_pairs={{0,8},{8,0},{1,9},{9,1},{2,10},{10,2},{3,11},{11,3},{4,12},{12,4},... | collective-permute-start | bytes 786440 | tf_op jit(solution)/shard_map/ppermute | solution.py:39
  28.5 1.1 %collective-permute-done.4.refs_5_ = bf16[16,8192]{1,0:T(8,128)(2,1)S(1)} collective-permute-done((bf16[16,8192]{1,0:T(8,128)(2,1)S(1)}, bf16[16,8192]{1,0:T(8,128)(2,1)S(1)}, u32[]{:S(2)}, u32[]{:S(2)}) %collective-permute-start.4) | collective-permute-done | bytes 262176 | tf_op jit(solution)/shard_map/ppermute | solution.py:35
  29.6 1.6 %collective-permute-start.12 = (bf16[16,8192]{1,0:T(8,128)(2,1)S(1)}, bf16[16,8192]{1,0:T(8,128)(2,1)S(1)}, u32[]{:S(2)}, u32[]{:S(2)}) collective-permute-start(bf16[16,8192]{1,0:T(8,128)(2,1)S(1)} %collective-permute-done.4.refs_5_), channel_id=1, source_target_pairs={{0,8},{8,0},{1,9},{9,1},{2,10},{10,2},{3,11},{11,3},{4,12},{12,4},... | collective-permute-start | bytes 786440 | tf_op jit(solution)/shard_map/ppermute | solution.py:39
  31.2 0.9 copy-done.1
  32.1 2.5 %widen.1.refs_17_.wide_ref = bf16[512,8192]{1,0:T(8,128)(2,1)S(1)} custom-call(s32[64,512]{1,0:T(8,128)S(1)} %bitcast.26), custom_call_target="tpu_custom_call" | custom-call | flops 10000000000 | bytes 30000000 | tf_op jit(solution)/shard_map/widen/pallas_call | solution.py:77
  34.6 0.0 copy-start.2
  34.6 0.0 collective-permute-done.9.refs_10_
  34.6 0.0 collective-permute-done.8.refs_9_
  34.6 0.0 collective-permute-done.12.refs_13_
  34.7 6.4 %forward.1 = f32[8,2,2,8,512]{4,3,2,1,0:T(8,128)S(1)} custom-call(bf16[16,8192]{1,0:T(8,128)(2,1)S(1)} %bitcast.24, bf16[16,8192]{1,0:T(8,128)(2,1)S(1)} %collective-permute-done.first.refs_1_, bf16[16,8192]{1,0:T(8,128)(2,1)S(1)} %collective-permute-done.1.second.refs_2_, bf16[16,8192]{1,0:T(8,128)(2,1)S(1)} %collective-permute-done.2.second.refs_3_, ...), custom_call_target="tpu_custom_call" | custom-call | flops 6000000000 | bytes 18000000 | tf_op jit(solution)/shard_map/forward/pallas_call | solution.py:135
  41.1 14.8 %all_to_all.10.parts = f32[8,2,2,8,512]{4,3,2,1,0:T(8,128)S(1)} all-to-all(f32[8,2,2,8,512]{4,3,2,1,0:T(8,128)S(1)} %forward.1), channel_id=1, replica_groups=mesh['xh'=2,'y'=4,'c'=2,'z'=4,'xl'=2] {'z','xl'}, dimensions={0} | all-to-all | bytes 1048576 | tf_op jit(solution)/shard_map/all_to_all | solution.py:299
  55.8 0.7 residual.1
  56.5 8.6 %all_to_all.11.every_ref = bf16[8,2,2,8,512]{4,3,2,1,0:T(8,128)(2,1)S(1)} all-to-all(bf16[8,2,2,8,512]{4,3,2,1,0:T(8,128)(2,1)S(1)} %get-tuple-element.39), channel_id=1, replica_groups=mesh['xh'=2,'y'=4,'c'=2,'z'=4,'xl'=2] {'z','xl'}, dimensions={0} | all-to-all | bytes 524288 | tf_op jit(solution)/shard_map/all_to_all | solution.py:301
  65.1 3.0 %backward.3 = (bf16[8,16,4096]{2,1,0:T(8,128)(2,1)S(1)}, bf16[2,16,4096]{2,1,0:T(8,128)(2,1)S(1)}, bf16[2,16,4096]{2,1,0:T(8,128)(2,1)S(1)}, bf16[2,16,4096]{2,1,0:T(8,128)(2,1)S(1)}, bf16[2,16,4096]{2,1,0:T(8,128)(2,1)S(1)}) custom-call(bf16[8,2,2,8,512]{4,3,2,1,0:T(8,128)(2,1)S(1)} %all_to_all.11.every_ref, bf16[2,512,8192]{2,1,0:T(8,128)(2,1)S(1)} %bitcast.18, ...), custom_call_target="tpu_custom_call" | custom-call | flops 3000000000 | bytes 9000000 | tf_op jit(solution)/shard_map/backward/pallas_call | solution.py:202
  68.0 2.4 %collective-permute-start.22 = (bf16[8,16,4096]{2,1,0:T(8,128)(2,1)S(1)}, bf16[8,16,4096]{2,1,0:T(8,128)(2,1)S(1)}, u32[]{:S(2)}, u32[]{:S(2)}) collective-permute-start(bf16[8,16,4096]{2,1,0:T(8,128)(2,1)S(1)} %get-tuple-element.57), channel_id=1, source_target_pairs={{0,8},{8,0},{1,9},{9,1},{2,10},{10,2},{3,11},{11,3},{4,12},{12,4},... | collective-permute-start | bytes 3145736 | tf_op jit(solution)/shard_map/ppermute | solution.py:39
  70.5 3.0 %backward.2 = (bf16[8,16,4096]{2,1,0:T(8,128)(2,1)S(1)}, bf16[2,16,4096]{2,1,0:T(8,128)(2,1)S(1)}, bf16[2,16,4096]{2,1,0:T(8,128)(2,1)S(1)}, bf16[2,16,4096]{2,1,0:T(8,128)(2,1)S(1)}, bf16[2,16,4096]{2,1,0:T(8,128)(2,1)S(1)}) custom-call(bf16[8,2,2,8,512]{4,3,2,1,0:T(8,128)(2,1)S(1)} %all_to_all.11.every_ref, bf16[2,512,8192]{2,1,0:T(8,128)(2,1)S(1)} %bitcast.18, ...), custom_call_target="tpu_custom_call" | custom-call | flops 3000000000 | bytes 9000000 | tf_op jit(solution)/shard_map/backward/pallas_call | solution.py:202
  73.4 0.1 collective-permute-start.15
  73.5 0.0 collective-permute-done.22.came
  73.5 0.2 chip_sum.3
  73.8 2.1 %collective-permute-start.23 = (bf16[2,16,4096]{2,1,0:T(8,128)(2,1)S(1)}, bf16[2,16,4096]{2,1,0:T(8,128)(2,1)S(1)}, u32[]{:S(2)}, u32[]{:S(2)}) collective-permute-start(bf16[2,16,4096]{2,1,0:T(8,128)(2,1)S(1)} %get-tuple-element.60), channel_id=1, source_target_pairs={{0,16},{8,72},{16,32},{24,88},{32,48},{40,104},{48,0},{56,120},{64... | collective-permute-start | bytes 786440 | tf_op jit(solution)/shard_map/ppermute | solution.py:35
  75.9 1.0 collective-permute-start.24
  76.8 0.7 collective-permute-start.25
  77.5 0.2 chip_sum.2
  77.8 2.2 %collective-permute-start.16 = (bf16[2,16,4096]{2,1,0:T(8,128)(2,1)S(1)}, bf16[2,16,4096]{2,1,0:T(8,128)(2,1)S(1)}, u32[]{:S(2)}, u32[]{:S(2)}) collective-permute-start(bf16[2,16,4096]{2,1,0:T(8,128)(2,1)S(1)} %get-tuple-element.47), channel_id=1, source_target_pairs={{0,16},{8,72},{16,32},{24,88},{32,48},{40,104},{48,0},{56,120},{64... | collective-permute-start | bytes 786440 | tf_op jit(solution)/shard_map/ppermute | solution.py:35
  80.0 1.0 collective-permute-start.17
  81.0 0.7 collective-permute-start.18
  81.7 1.7 %collective-permute-done.24.q2 = bf16[2,16,4096]{2,1,0:T(8,128)(2,1)S(1)} collective-permute-done((bf16[2,16,4096]{2,1,0:T(8,128)(2,1)S(1)}, bf16[2,16,4096]{2,1,0:T(8,128)(2,1)S(1)}, u32[]{:S(2)}, u32[]{:S(2)}) %collective-permute-start.24) | collective-permute-done | bytes 262176 | tf_op jit(solution)/shard_map/ppermute | solution.py:35
  83.4 0.1 stage_sum.3
  83.5 0.1 collective-permute-start.26
  83.6 4.6 %collective-permute-start.27 = (bf16[16,4096]{1,0:T(8,128)(2,1)S(1)}, bf16[16,4096]{1,0:T(8,128)(2,1)S(1)}, u32[]{:S(2)}, u32[]{:S(2)}) collective-permute-start(bf16[16,4096]{1,0:T(8,128)(2,1)S(1)} %get-tuple-element.64), channel_id=1, source_target_pairs={{8,56},{24,8},{40,24},{56,40},{72,120},{88,72},{104,88},{120,104},... | collective-permute-start | bytes 393224 | tf_op jit(solution)/shard_map/ppermute | solution.py:35
  88.2 0.0 collective-permute-done.16.q1
  88.2 1.9 %collective-permute-start.28 = (bf16[16,4096]{1,0:T(8,128)(2,1)S(1)}, bf16[16,4096]{1,0:T(8,128)(2,1)S(1)}, u32[]{:S(2)}, u32[]{:S(2)}) collective-permute-start(bf16[16,4096]{1,0:T(8,128)(2,1)S(1)} %get-tuple-element.65), channel_id=1, source_target_pairs={{8,40},{24,56},{40,8},{56,24},{72,104},{88,120},{104,72},{120,88},... | collective-permute-start | bytes 393224 | tf_op jit(solution)/shard_map/ppermute | solution.py:35
  90.1 0.1 stage_sum.2
  90.3 0.6 collective-permute-start.19
  90.9 4.0 %collective-permute-start.20 = (bf16[16,4096]{1,0:T(8,128)(2,1)S(1)}, bf16[16,4096]{1,0:T(8,128)(2,1)S(1)}, u32[]{:S(2)}, u32[]{:S(2)}) collective-permute-start(bf16[16,4096]{1,0:T(8,128)(2,1)S(1)} %get-tuple-element.51), channel_id=1, source_target_pairs={{8,56},{24,8},{40,24},{56,40},{72,120},{88,72},{104,88},{120,104},... | collective-permute-start | bytes 393224 | tf_op jit(solution)/shard_map/ppermute | solution.py:35
  94.9 3.7 %collective-permute-start.21 = (bf16[16,4096]{1,0:T(8,128)(2,1)S(1)}, bf16[16,4096]{1,0:T(8,128)(2,1)S(1)}, u32[]{:S(2)}, u32[]{:S(2)}) collective-permute-start(bf16[16,4096]{1,0:T(8,128)(2,1)S(1)} %get-tuple-element.52), channel_id=1, source_target_pairs={{8,40},{24,56},{40,8},{56,24},{72,104},{88,120},{104,72},{120,88},... | collective-permute-start | bytes 393224 | tf_op jit(solution)/shard_map/ppermute | solution.py:35
  98.6 0.1 fusion.1
  98.7 3.4 %collective-permute-done.21 = bf16[16,4096]{1,0:T(8,128)(2,1)S(1)} collective-permute-done((bf16[16,4096]{1,0:T(8,128)(2,1)S(1)}, bf16[16,4096]{1,0:T(8,128)(2,1)S(1)}, u32[]{:S(2)}, u32[]{:S(2)}) %collective-permute-start.21) | collective-permute-done | bytes 131104 | tf_op jit(solution)/shard_map/ppermute | solution.py:35
  102.2 0.1 fusion
  102.2 0.7 maximum_bitcast_fusion
  (27 shorter events, 0.1 us)
Async XLA Ops:
  0.6 11.7 %collective-permute-start = (bf16[16,8192]{1,0:T(8,128)(2,1)}, bf16[16,8192]{1,0:T(8,128)(2,1)S(1)}, u32[]{:S(2)}, u32[]{:S(2)}) collective-permute-start(bf16[16,8192]{1,0:T(8,128)(2,1)} %bitcast.19), channel_id=1, source_target_pairs={{0,64},{8,24},{16,80},{24,40},{32,96},{40,56},{48,112},{56,8},{64,... | collective-permute-start | bytes 786440 | tf_op jit(solution)/shard_map/ppermute | solution.py:35
  2.8 9.5 %collective-permute-start.1 = (bf16[16,8192]{1,0:T(8,128)(2,1)}, bf16[16,8192]{1,0:T(8,128)(2,1)S(1)}, u32[]{:S(2)}, u32[]{:S(2)}) collective-permute-start(bf16[16,8192]{1,0:T(8,128)(2,1)} %bitcast.20), channel_id=1, source_target_pairs={{0,16},{8,56},{16,32},{24,8},{32,48},{40,24},{48,0},{56,40},{64,80... | collective-permute-start | bytes 786440 | tf_op jit(solution)/shard_map/ppermute | solution.py:35
  4.3 11.8 %collective-permute-start.3 = (bf16[16,8192]{1,0:T(8,128)(2,1)}, bf16[16,8192]{1,0:T(8,128)(2,1)S(1)}, u32[]{:S(2)}, u32[]{:S(2)}) collective-permute-start(bf16[16,8192]{1,0:T(8,128)(2,1)} %bitcast.21), channel_id=1, source_target_pairs={{0,32},{8,72},{16,48},{24,88},{32,0},{40,104},{48,16},{56,120},{64... | collective-permute-start | bytes 786440 | tf_op jit(solution)/shard_map/ppermute | solution.py:35
  7.1 12.8 %collective-permute-start.2 = (bf16[16,8192]{1,0:T(8,128)(2,1)}, bf16[16,8192]{1,0:T(8,128)(2,1)S(1)}, u32[]{:S(2)}, u32[]{:S(2)}) collective-permute-start(bf16[16,8192]{1,0:T(8,128)(2,1)} %bitcast.22), channel_id=1, source_target_pairs={{0,48},{8,40},{16,0},{24,56},{32,16},{40,8},{48,32},{56,24},{64,11... | collective-permute-start | bytes 786440 | tf_op jit(solution)/shard_map/ppermute | solution.py:35
  8.6 12.8 %collective-permute-start.7 = (bf16[16,8192]{1,0:T(8,128)(2,1)}, bf16[16,8192]{1,0:T(8,128)(2,1)S(1)}, u32[]{:S(2)}, u32[]{:S(2)}) collective-permute-start(bf16[16,8192]{1,0:T(8,128)(2,1)} %bitcast.23), channel_id=1, source_target_pairs={{0,8},{8,0},{1,9},{9,1},{2,10},{10,2},{3,11},{11,3},{4,12},{12,4},... | collective-permute-start | bytes 786440 | tf_op jit(solution)/shard_map/ppermute | solution.py:39
  12.3 11.2 %collective-permute-start.5 = (bf16[16,8192]{1,0:T(8,128)(2,1)S(1)}, bf16[16,8192]{1,0:T(8,128)(2,1)S(1)}, u32[]{:S(2)}, u32[]{:S(2)}) collective-permute-start(bf16[16,8192]{1,0:T(8,128)(2,1)S(1)} %pick.2), channel_id=1, source_target_pairs={{0,48},{8,72},{16,0},{24,88},{32,16},{40,104},{48,32},{56,120},{64... | collective-permute-start | bytes 786440 | tf_op jit(solution)/shard_map/ppermute | solution.py:35
  16.2 6.8 %collective-permute-start.11 = (bf16[16,8192]{1,0:T(8,128)(2,1)S(1)}, bf16[16,8192]{1,0:T(8,128)(2,1)S(1)}, u32[]{:S(2)}, u32[]{:S(2)}) collective-permute-start(bf16[16,8192]{1,0:T(8,128)(2,1)S(1)} %collective-permute-done.3.refs_4_), channel_id=1, source_target_pairs={{0,8},{8,0},{1,9},{9,1},{2,10},{10,2},{3,11},{11,3},{4,12},{12,4},... | collective-permute-start | bytes 786440 | tf_op jit(solution)/shard_map/ppermute | solution.py:39
  19.9 3.2 %collective-permute-start.10 = (bf16[16,8192]{1,0:T(8,128)(2,1)S(1)}, bf16[16,8192]{1,0:T(8,128)(2,1)S(1)}, u32[]{:S(2)}, u32[]{:S(2)}) collective-permute-start(bf16[16,8192]{1,0:T(8,128)(2,1)S(1)} %collective-permute-done.2.second.refs_3_), channel_id=1, source_target_pairs={{0,8},{8,0},{1,9},{9,1},{2,10},{10,2},{3,11},{11,3},{4,12},{12,4},... | collective-permute-start | bytes 786440 | tf_op jit(solution)/shard_map/ppermute | solution.py:39
  19.9 14.8 %slice-start = ((s8[16777216]{0:T(1024)(128)(4,1)}), s8[4194304]{0:T(1024)(128)(4,1)S(1)}, s32[]{:S(2)}) async-start(s8[16777216]{0:T(1024)(128)(4,1)} %bitcast.17), calls=%async_computation.2 | async-start | bytes 8388608
  19.9 14.7 %slice-start.1 = ((s8[16777216]{0:T(1024)(128)(4,1)}), s8[4194304]{0:T(1024)(128)(4,1)S(1)}, s32[]{:S(2)}) async-start(s8[16777216]{0:T(1024)(128)(4,1)} %bitcast.17), calls=%async_computation.3 | async-start | bytes 8388608
  19.9 14.7 %slice-start.2 = ((s8[16777216]{0:T(1024)(128)(4,1)}), s8[4194304]{0:T(1024)(128)(4,1)S(1)}, s32[]{:S(2)}) async-start(s8[16777216]{0:T(1024)(128)(4,1)} %bitcast.17), calls=%async_computation.4 | async-start | bytes 8388608
  19.9 14.7 %slice-start.3 = ((s8[16777216]{0:T(1024)(128)(4,1)}), s8[4194304]{0:T(1024)(128)(4,1)S(1)}, s32[]{:S(2)}) async-start(s8[16777216]{0:T(1024)(128)(4,1)} %bitcast.17), calls=%async_computation.5 | async-start | bytes 8388608
  20.0 14.7 %copy-start = (bf16[2,8192,8]{1,2,0:T(8,128)(2,1)S(1)}, bf16[2,8192,8]{1,2,0:T(8,128)(2,1)}, u32[]{:S(2)}) copy-start(bf16[2,8192,8]{1,2,0:T(8,128)(2,1)} %param.7) | copy-start | bytes 786436
  20.0 7.1 %collective-permute-start.6 = (bf16[16,8192]{1,0:T(8,128)(2,1)S(1)}, bf16[16,8192]{1,0:T(8,128)(2,1)S(1)}, u32[]{:S(2)}, u32[]{:S(2)}) collective-permute-start(bf16[16,8192]{1,0:T(8,128)(2,1)S(1)} %pick.3), channel_id=1, source_target_pairs={{0,32},{8,72},{16,48},{24,88},{32,0},{40,104},{48,16},{56,120},{64... | collective-permute-start | bytes 786440 | tf_op jit(solution)/shard_map/ppermute | solution.py:35
  21.4 8.1 %collective-permute-start.4 = (bf16[16,8192]{1,0:T(8,128)(2,1)S(1)}, bf16[16,8192]{1,0:T(8,128)(2,1)S(1)}, u32[]{:S(2)}, u32[]{:S(2)}) collective-permute-start(bf16[16,8192]{1,0:T(8,128)(2,1)S(1)} %collective-permute-done.first.refs_1_), channel_id=1, source_target_pairs={{0,16},{8,72},{16,32},{24,88},{32,48},{40,104},{48,0},{56,120},{64... | collective-permute-start | bytes 786440 | tf_op jit(solution)/shard_map/ppermute | solution.py:35
  23.0 11.6 %collective-permute-start.8 = (bf16[16,8192]{1,0:T(8,128)(2,1)S(1)}, bf16[16,8192]{1,0:T(8,128)(2,1)S(1)}, u32[]{:S(2)}, u32[]{:S(2)}) collective-permute-start(bf16[16,8192]{1,0:T(8,128)(2,1)S(1)} %collective-permute-done.first.refs_1_), channel_id=1, source_target_pairs={{0,8},{8,0},{1,9},{9,1},{2,10},{10,2},{3,11},{11,3},{4,12},{12,4},... | collective-permute-start | bytes 786440 | tf_op jit(solution)/shard_map/ppermute | solution.py:39
  23.0 11.6 %collective-permute-start.9 = (bf16[16,8192]{1,0:T(8,128)(2,1)S(1)}, bf16[16,8192]{1,0:T(8,128)(2,1)S(1)}, u32[]{:S(2)}, u32[]{:S(2)}) collective-permute-start(bf16[16,8192]{1,0:T(8,128)(2,1)S(1)} %collective-permute-done.1.second.refs_2_), channel_id=1, source_target_pairs={{0,8},{8,0},{1,9},{9,1},{2,10},{10,2},{3,11},{11,3},{4,12},{12,4},... | collective-permute-start | bytes 786440 | tf_op jit(solution)/shard_map/ppermute | solution.py:39
  23.5 11.1 %collective-permute-start.13 = (bf16[16,8192]{1,0:T(8,128)(2,1)S(1)}, bf16[16,8192]{1,0:T(8,128)(2,1)S(1)}, u32[]{:S(2)}, u32[]{:S(2)}) collective-permute-start(bf16[16,8192]{1,0:T(8,128)(2,1)S(1)} %collective-permute-done.5.refs_6_), channel_id=1, source_target_pairs={{0,8},{8,0},{1,9},{9,1},{2,10},{10,2},{3,11},{11,3},{4,12},{12,4},... | collective-permute-start | bytes 786440 | tf_op jit(solution)/shard_map/ppermute | solution.py:39
  27.1 7.6 %collective-permute-start.14 = (bf16[16,8192]{1,0:T(8,128)(2,1)S(1)}, bf16[16,8192]{1,0:T(8,128)(2,1)S(1)}, u32[]{:S(2)}, u32[]{:S(2)}) collective-permute-start(bf16[16,8192]{1,0:T(8,128)(2,1)S(1)} %collective-permute-done.6.refs_7_), channel_id=1, source_target_pairs={{0,8},{8,0},{1,9},{9,1},{2,10},{10,2},{3,11},{11,3},{4,12},{12,4},... | collective-permute-start | bytes 786440 | tf_op jit(solution)/shard_map/ppermute | solution.py:39
  29.6 5.1 %collective-permute-start.12 = (bf16[16,8192]{1,0:T(8,128)(2,1)S(1)}, bf16[16,8192]{1,0:T(8,128)(2,1)S(1)}, u32[]{:S(2)}, u32[]{:S(2)}) collective-permute-start(bf16[16,8192]{1,0:T(8,128)(2,1)S(1)} %collective-permute-done.4.refs_5_), channel_id=1, source_target_pairs={{0,8},{8,0},{1,9},{9,1},{2,10},{10,2},{3,11},{11,3},{4,12},{12,4},... | collective-permute-start | bytes 786440 | tf_op jit(solution)/shard_map/ppermute | solution.py:39
  31.2 0.9 copy-start.1
  34.6 21.3 %copy-start.2 = (s32[512]{0:T(512)S(1)}, s32[512]{0:T(512)}, u32[]{:S(2)}) copy-start(s32[512]{0:T(512)} %param.9) | copy-start | bytes 6148
  68.0 5.5 %collective-permute-start.22 = (bf16[8,16,4096]{2,1,0:T(8,128)(2,1)S(1)}, bf16[8,16,4096]{2,1,0:T(8,128)(2,1)S(1)}, u32[]{:S(2)}, u32[]{:S(2)}) collective-permute-start(bf16[8,16,4096]{2,1,0:T(8,128)(2,1)S(1)} %get-tuple-element.57), channel_id=1, source_target_pairs={{0,8},{8,0},{1,9},{9,1},{2,10},{10,2},{3,11},{11,3},{4,12},{12,4},... | collective-permute-start | bytes 3145736 | tf_op jit(solution)/shard_map/ppermute | solution.py:39
  73.4 4.1 %collective-permute-start.15 = (bf16[8,16,4096]{2,1,0:T(8,128)(2,1)S(1)}, bf16[8,16,4096]{2,1,0:T(8,128)(2,1)S(1)}, u32[]{:S(2)}, u32[]{:S(2)}) collective-permute-start(bf16[8,16,4096]{2,1,0:T(8,128)(2,1)S(1)} %get-tuple-element.44), channel_id=1, source_target_pairs={{0,8},{8,0},{1,9},{9,1},{2,10},{10,2},{3,11},{11,3},{4,12},{12,4},... | collective-permute-start | bytes 3145736 | tf_op jit(solution)/shard_map/ppermute | solution.py:39
  73.8 7.2 %collective-permute-start.23 = (bf16[2,16,4096]{2,1,0:T(8,128)(2,1)S(1)}, bf16[2,16,4096]{2,1,0:T(8,128)(2,1)S(1)}, u32[]{:S(2)}, u32[]{:S(2)}) collective-permute-start(bf16[2,16,4096]{2,1,0:T(8,128)(2,1)S(1)} %get-tuple-element.60), channel_id=1, source_target_pairs={{0,16},{8,72},{16,32},{24,88},{32,48},{40,104},{48,0},{56,120},{64... | collective-permute-start | bytes 786440 | tf_op jit(solution)/shard_map/ppermute | solution.py:35
  75.9 7.5 %collective-permute-start.24 = (bf16[2,16,4096]{2,1,0:T(8,128)(2,1)S(1)}, bf16[2,16,4096]{2,1,0:T(8,128)(2,1)S(1)}, u32[]{:S(2)}, u32[]{:S(2)}) collective-permute-start(bf16[2,16,4096]{2,1,0:T(8,128)(2,1)S(1)} %get-tuple-element.61), channel_id=1, source_target_pairs={{0,48},{8,72},{16,0},{24,88},{32,16},{40,104},{48,32},{56,120},{64... | collective-permute-start | bytes 786440 | tf_op jit(solution)/shard_map/ppermute | solution.py:35
  76.8 6.6 %collective-permute-start.25 = (bf16[2,16,4096]{2,1,0:T(8,128)(2,1)S(1)}, bf16[2,16,4096]{2,1,0:T(8,128)(2,1)S(1)}, u32[]{:S(2)}, u32[]{:S(2)}) collective-permute-start(bf16[2,16,4096]{2,1,0:T(8,128)(2,1)S(1)} %get-tuple-element.58.u3), channel_id=1, source_target_pairs={{0,32},{16,48},{32,0},{48,16},{64,96},{80,112},{96,64},{112,80},{1... | collective-permute-start | bytes 786440 | tf_op jit(solution)/shard_map/ppermute | solution.py:35
  77.8 10.4 %collective-permute-start.16 = (bf16[2,16,4096]{2,1,0:T(8,128)(2,1)S(1)}, bf16[2,16,4096]{2,1,0:T(8,128)(2,1)S(1)}, u32[]{:S(2)}, u32[]{:S(2)}) collective-permute-start(bf16[2,16,4096]{2,1,0:T(8,128)(2,1)S(1)} %get-tuple-element.47), channel_id=1, source_target_pairs={{0,16},{8,72},{16,32},{24,88},{32,48},{40,104},{48,0},{56,120},{64... | collective-permute-start | bytes 786440 | tf_op jit(solution)/shard_map/ppermute | solution.py:35
  80.0 10.1 %collective-permute-start.17 = (bf16[2,16,4096]{2,1,0:T(8,128)(2,1)S(1)}, bf16[2,16,4096]{2,1,0:T(8,128)(2,1)S(1)}, u32[]{:S(2)}, u32[]{:S(2)}) collective-permute-start(bf16[2,16,4096]{2,1,0:T(8,128)(2,1)S(1)} %get-tuple-element.48), channel_id=1, source_target_pairs={{0,48},{8,72},{16,0},{24,88},{32,16},{40,104},{48,32},{56,120},{64... | collective-permute-start | bytes 786440 | tf_op jit(solution)/shard_map/ppermute | solution.py:35
  81.0 9.1 %collective-permute-start.18 = (bf16[2,16,4096]{2,1,0:T(8,128)(2,1)S(1)}, bf16[2,16,4096]{2,1,0:T(8,128)(2,1)S(1)}, u32[]{:S(2)}, u32[]{:S(2)}) collective-permute-start(bf16[2,16,4096]{2,1,0:T(8,128)(2,1)S(1)} %get-tuple-element.45.u3), channel_id=1, source_target_pairs={{0,32},{16,48},{32,0},{48,16},{64,96},{80,112},{96,64},{112,80},{1... | collective-permute-start | bytes 786440 | tf_op jit(solution)/shard_map/ppermute | solution.py:35
  83.5 11.4 %collective-permute-start.26 = (bf16[16,4096]{1,0:T(8,128)(2,1)S(1)}, bf16[16,4096]{1,0:T(8,128)(2,1)S(1)}, u32[]{:S(2)}, u32[]{:S(2)}) collective-permute-start(bf16[16,4096]{1,0:T(8,128)(2,1)S(1)} %get-tuple-element.63), channel_id=1, source_target_pairs={{0,64},{8,24},{16,80},{24,40},{32,96},{40,56},{48,112},{56,8},{64,... | collective-permute-start | bytes 393224 | tf_op jit(solution)/shard_map/ppermute | solution.py:35
  83.6 15.0 %collective-permute-start.27 = (bf16[16,4096]{1,0:T(8,128)(2,1)S(1)}, bf16[16,4096]{1,0:T(8,128)(2,1)S(1)}, u32[]{:S(2)}, u32[]{:S(2)}) collective-permute-start(bf16[16,4096]{1,0:T(8,128)(2,1)S(1)} %get-tuple-element.64), channel_id=1, source_target_pairs={{8,56},{24,8},{40,24},{56,40},{72,120},{88,72},{104,88},{120,104},... | collective-permute-start | bytes 393224 | tf_op jit(solution)/shard_map/ppermute | solution.py:35
  88.2 10.4 %collective-permute-start.28 = (bf16[16,4096]{1,0:T(8,128)(2,1)S(1)}, bf16[16,4096]{1,0:T(8,128)(2,1)S(1)}, u32[]{:S(2)}, u32[]{:S(2)}) collective-permute-start(bf16[16,4096]{1,0:T(8,128)(2,1)S(1)} %get-tuple-element.65), channel_id=1, source_target_pairs={{8,40},{24,56},{40,8},{56,24},{72,104},{88,120},{104,72},{120,88},... | collective-permute-start | bytes 393224 | tf_op jit(solution)/shard_map/ppermute | solution.py:35
  90.3 8.4 %collective-permute-start.19 = (bf16[16,4096]{1,0:T(8,128)(2,1)S(1)}, bf16[16,4096]{1,0:T(8,128)(2,1)S(1)}, u32[]{:S(2)}, u32[]{:S(2)}) collective-permute-start(bf16[16,4096]{1,0:T(8,128)(2,1)S(1)} %get-tuple-element.50), channel_id=1, source_target_pairs={{0,64},{8,24},{16,80},{24,40},{32,96},{40,56},{48,112},{56,8},{64,... | collective-permute-start | bytes 393224 | tf_op jit(solution)/shard_map/ppermute | solution.py:35
  90.9 7.8 %collective-permute-start.20 = (bf16[16,4096]{1,0:T(8,128)(2,1)S(1)}, bf16[16,4096]{1,0:T(8,128)(2,1)S(1)}, u32[]{:S(2)}, u32[]{:S(2)}) collective-permute-start(bf16[16,4096]{1,0:T(8,128)(2,1)S(1)} %get-tuple-element.51), channel_id=1, source_target_pairs={{8,56},{24,8},{40,24},{56,40},{72,120},{88,72},{104,88},{120,104},... | collective-permute-start | bytes 393224 | tf_op jit(solution)/shard_map/ppermute | solution.py:35
  94.9 7.2 %collective-permute-start.21 = (bf16[16,4096]{1,0:T(8,128)(2,1)S(1)}, bf16[16,4096]{1,0:T(8,128)(2,1)S(1)}, u32[]{:S(2)}, u32[]{:S(2)}) collective-permute-start(bf16[16,4096]{1,0:T(8,128)(2,1)S(1)} %get-tuple-element.52), channel_id=1, source_target_pairs={{8,40},{24,56},{40,8},{56,24},{72,104},{88,120},{104,72},{120,88},... | collective-permute-start | bytes 393224 | tf_op jit(solution)/shard_map/ppermute | solution.py:35

commit v3 on v2

--- a/solution.py
+++ b/solution.py
@@ -63,26 +63,32 @@
     return jnp.concatenate([codes_ref[0, :, cols] * wide, codes_ref[1, :, cols] * wide], axis=0)
 
 
-def widen_body(exps_ref, wide_ref):
+def prepare_body(exps_ref, observed_ref, wide_ref, seen_ref, turn_ref):
     exps = exps_ref[...]
     scale = jnp.where(exps >= -14, 2.0**-14, jnp.where(exps == -15, 2.0**-15, jnp.where(exps == -16, 2.0**-16, 2.0**-17)))
     scale = scale.astype(jnp.float32).T
     for b in range(exps.shape[0]):
         wide = jnp.broadcast_to(scale[:, b : b + 1], (scale.shape[0], EXP_BLOCK)).astype(jnp.bfloat16)
         wide_ref[:, b * EXP_BLOCK : (b + 1) * EXP_BLOCK] = wide
-
-
-def widen(exps):
+    share = lax.axis_index("z") * 2 + lax.axis_index("xl")
+    for k in range(2):
+        turn_ref[...] = observed_ref[k].astype(jnp.float32).T
+        for c in range(2):
+            seen_ref[k, c] = turn_ref[pl.ds(pl.multiple_of(share * 16 + c * 8, 8), 8), :]
+
+
+def prepare(exps, observed):
     blocks, rows = exps.shape
     return pl.pallas_call(
-        widen_body,
-        in_specs=[VM],
-        out_specs=VM,
-        out_shape=pltpu.VMEM((rows, blocks * EXP_BLOCK), jnp.bfloat16),
-        cost_estimate=cost(10),
-        compiler_params=params(4),
-        name="widen",
-    )(exps)
+        prepare_body,
+        in_specs=[VM] * 2,
+        out_specs=[VM] * 2,
+        out_shape=[pltpu.VMEM((rows, blocks * EXP_BLOCK), jnp.bfloat16), pltpu.VMEM((2, 2, 8, rows), jnp.float32)],
+        scratch_shapes=[pltpu.VMEM((observed.shape[2], rows), jnp.float32)],
+        cost_estimate=cost(4),
+        compiler_params=params(6),
+        name="prepare",
+    )(exps, observed)
 
 
 def pick_body(first, second, out):
@@ -103,7 +109,7 @@
         in_specs=[VM] * 2,
         out_specs=VM,
         out_shape=jax.ShapeDtypeStruct(first.shape, first.dtype),
-        cost_estimate=cost(1),
+        cost_estimate=cost(8),
         compiler_params=params(4),
         name="pick",
     )(first, second)
@@ -130,7 +136,7 @@
             out_ref[at, c, 1] = im[:, :rows] + re[:, rows:]
 
 
-def forward(pieces, codes, wide, tile=1024):
+def forward(pieces, codes, wide, tile=8192):
     rows = codes.shape[1]
     return pl.pallas_call(
         functools.partial(forward_body, tile, rows),
@@ -172,41 +178,38 @@
     )(parts, seen, mask)
 
 
-def backward_body(start, tile, every_ref, codes_ref, wide_ref, *refs):
-    other_ref, mine, a_ref = refs[0], refs[1:5], refs[5]
+def backward_body(which, tile, every_ref, codes_ref, wide_ref, *refs):
+    outs, a_ref = refs[:-1], refs[-1]
     rows = codes_ref.shape[1]
-    core = lax.axis_index("c")
-    for k in range(16):
-        block = every_ref[here(lax.bitwise_xor(core, k // 8), DEST, k % 8), k // 8].astype(jnp.float32)
+    owner = lax.bitwise_xor(lax.axis_index("c"), which)
+    for k in range(8):
+        block = every_ref[here(owner, DEST, k), which].astype(jnp.float32)
         top = slice(16 * k, 16 * k + 16)
         a_ref[top, :rows] = jnp.concatenate([block[0], block[1]], axis=0).astype(jnp.bfloat16)
         a_ref[top, rows:] = jnp.concatenate([block[1], -block[0]], axis=0).astype(jnp.bfloat16)
 
     def step(i, _):
-        at = pl.multiple_of(start + i * tile, tile)
-        to = pl.ds(pl.multiple_of(i * tile, tile), tile)
-        kern = decode(codes_ref, wide_ref, pl.ds(at, tile))
+        cols = pl.ds(pl.multiple_of(i * tile, tile), tile)
+        kern = decode(codes_ref, wide_ref, cols)
         prod = jnp.dot(a_ref[...], kern, preferred_element_type=jnp.float32).astype(jnp.bfloat16)
+        each = 8 // len(outs)
         for k in range(8):
-            mine[k // 2][k % 2, :, to] = prod[16 * k : 16 * k + 16]
-            other_ref[k, :, to] = prod[128 + 16 * k : 144 + 16 * k]
+            outs[k // each][k % each, :, cols] = prod[16 * k : 16 * k + 16]
         return 0
 
-    lax.fori_loop(0, other_ref.shape[2] // tile, step, 0)
-
-
-def backward(every, codes, wide, part, parts, tile=1024):
+    lax.fori_loop(0, codes_ref.shape[2] // tile, step, 0)
+
+
+def backward(every, codes, wide, which, count, tile=8192):
     _, rows, cols = codes.shape
-    cols = cols // parts
-    pair = jax.ShapeDtypeStruct((2, 16, cols), jnp.bfloat16)
-    return pl.pallas_call(
-        functools.partial(backward_body, part * cols, tile),
+    return pl.pallas_call(
+        functools.partial(backward_body, which, tile),
         in_specs=[VM] * 3,
-        out_specs=[VM] * 5,
-        out_shape=[jax.ShapeDtypeStruct((8, 16, cols), jnp.bfloat16)] + [pair] * 4,
-        scratch_shapes=[pltpu.VMEM((256, 2 * rows), jnp.bfloat16)],
+        out_specs=[VM] * count,
+        out_shape=[jax.ShapeDtypeStruct((8 // count, 16, cols), jnp.bfloat16)] * count,
+        scratch_shapes=[pltpu.VMEM((128, 2 * rows), jnp.bfloat16)],
         cost_estimate=cost(3),
-        compiler_params=params(10),
+        compiler_params=params(8),
         name="backward",
     )(every, vmem(codes), vmem(wide))
 
@@ -263,16 +266,15 @@
     )(u3, u4, q1, q2, q3)
 
 
-def gather(own, ready):
+def gather(own):
     r1 = move(own, X, Y1)
     r2 = move(own, Y1, Y3)
     r3 = move(own, Y3, Y2)
     r4 = move(own, Y2, X)
-    r1, ready = lax.optimization_barrier((r1, ready))
     r5 = move(r1, Y1, X)
     r6 = move(pick(r1, r2), Y3, X)
     r7 = move(pick(r1, r3), Y2, X)
-    return [own, r1, r2, r3, r4, r5, r6, r7], ready
+    return [own, r1, r2, r3, r4, r5, r6, r7]
 
 
 def scatter(mine, came):
@@ -290,21 +292,18 @@
 def body(codes, exps, wavefield, observed, mask):
     _, rows, cols = codes.shape
     own = wavefield.transpose(0, 2, 1).reshape(16, cols)
-    seen = lax.dynamic_slice_in_dim(observed, lax.axis_index(SRC) * 16, 16, 2)
-    seen = seen.astype(jnp.float32).transpose(0, 2, 1).reshape(2, 2, 8, rows)
-    pieces, (exps, seen, mask) = gather(own, (exps.T, seen, mask.reshape(1, rows)))
-    wide = widen(exps)
+    pieces = gather(own)
+    wide, seen = prepare(exps.T, observed)
     pieces += [swap(p) for p in pieces]
     parts = forward(pieces, codes, wide)
     parts = lax.all_to_all(parts, SRC, 0, 0, tiled=True)
-    every, own_resid = residual(parts, seen, mask)
+    every, own_resid = residual(parts, vmem(seen), mask.reshape(1, rows))
     every = lax.all_to_all(every, SRC, 0, 0, tiled=True)
-    halves = []
-    for part in range(2):
-        other, *mine = backward(every, codes, wide, part, 2)
-        halves.append((mine, swap(other)))
-    sums = [scatter(mine, came) for mine, came in halves]
-    gradient = jnp.concatenate(sums, axis=1).astype(jnp.bfloat16).reshape(2, 8, cols)
+    (other,) = backward(every, codes, wide, 1, 1)
+    came = swap(other)
+    mine = backward(every, codes, wide, 0, 4)
+    gradient = scatter(mine, came)
+    gradient = gradient.astype(jnp.bfloat16).reshape(2, 8, cols)
     return own_resid.reshape(2, 16, rows).transpose(0, 2, 1), gradient.transpose(0, 2, 1)
 
 

time: 103 us -> 102 us (level)
  waiting for transfers between devices: 9.75 us -> 26.6 us
  starting transfers between devices: 49.6 us -> 35.9 us
  Pallas kernels: 16.2 us -> 13.4 us
  other arithmetic: 1.93 us -> 0.82 us
  local copies, waits for them, and re-layouts: 1.1 us -> 0.04 us
    ppermute x19 -> x13, waiting for transfers between devices: 9.72 us -> 25.2 us  [move(): return lax.ppermute(x, RCV, pairs)]
    ppermute x19 -> x13, starting transfers between devices: 37.3 us -> 23.2 us  [move(): return lax.ppermute(x, RCV, pairs)]
    pallas_call x1, Pallas kernels: 6.37 us -> 4.61 us  [forward(): pl.pallas_call(functools.partial(forward_body, tile, rows), in_specs=[VM]...]
    ppermute x10 -> x9, waiting for transfers between devices: 0.03 us -> 1.38 us  [swap(): return lax.ppermute(x, 'c', SWAP)]
    reshape x1 -> x0, other arithmetic: 1.08 us -> none  [body(): seen = seen.astype(jnp.float32).transpose(0, 2, 1).reshape(2, 2, 8, rows)]
    ppermute x10 -> x9, starting transfers between devices: 12.3 us -> 12.7 us  [swap(): return lax.ppermute(x, 'c', SWAP)]
  transfers between devices with their start and end apart: 29 -> 22, of which waited for: 4 -> 8; matrix products, arithmetic and copies ran while one was open for 1% -> 0% of each run, Pallas kernels for 6% -> 5%
where the time goes in v3:
time: 102 us
  starting transfers between devices  35.9 us (35%)
  waiting for transfers between devices  26.6 us (26%)
  blocking collectives  24.1 us (24%)
  Pallas kernels  13.4 us (13%)
    ppermute x13, waiting for transfers between devices, move(): return lax.ppermute(x, RCV, pairs)  25.2 us
    ppermute x13, starting transfers between devices, move(): return lax.ppermute(x, RCV, pairs)  23.2 us
    all_to_all x1, blocking collectives, body(): parts = lax.all_to_all(parts, SRC, 0, 0, tiled=True)  15.6 us
    ppermute x9, starting transfers between devices, swap(): return lax.ppermute(x, 'c', SWAP)  12.7 us
    all_to_all x1, blocking collectives, body(): every = lax.all_to_all(every, SRC, 0, 0, tiled=True)  8.57 us
    pallas_call x2, Pallas kernels, backward(): pl.pallas_call(functools.partial(backward_body, which, tile), in_specs=[V...  4.81 us
    pallas_call x1, Pallas kernels, forward(): pl.pallas_call(functools.partial(forward_body, tile, rows), in_specs=[VM]...  4.61 us
    pallas_call x1, Pallas kernels, prepare(): pl.pallas_call(prepare_body, in_specs=[VM] * 2, out_specs=[VM] * 2, out_s...  2.55 us
  transfers between devices with their start and end apart: 22, of which 8 were waited for; matrix products, arithmetic and copies ran while one was open for 0% of the time, Pallas kernels for 5%

profile of v3, /device:TPU:1, one launch (start us, length us, event | category | flops | bytes accessed | tf_op | source)
XLA Modules:
  0.0 101.7 jit_solution(8422152521148596580)
XLA Ops:
  0.6 3.6 %collective-permute-start.1 = (bf16[16,8192]{1,0:T(8,128)(2,1)}, bf16[16,8192]{1,0:T(8,128)(2,1)S(1)}, u32[]{:S(2)}, u32[]{:S(2)}) collective-permute-start(bf16[16,8192]{1,0:T(8,128)(2,1)} %bitcast.14), channel_id=1, source_target_pairs={{0,16},{8,56},{16,32},{24,8},{32,48},{40,24},{48,0},{56,40},{64,80... | collective-permute-start | bytes 786440 | tf_op jit(solution)/shard_map/ppermute | solution.py:35
  4.2 0.0 collective-permute-start
  4.3 2.5 %collective-permute-start.7 = (bf16[16,8192]{1,0:T(8,128)(2,1)}, bf16[16,8192]{1,0:T(8,128)(2,1)S(1)}, u32[]{:S(2)}, u32[]{:S(2)}) collective-permute-start(bf16[16,8192]{1,0:T(8,128)(2,1)} %bitcast.16), channel_id=1, source_target_pairs={{0,8},{8,0},{1,9},{9,1},{2,10},{10,2},{3,11},{11,3},{4,12},{12,4},... | collective-permute-start | bytes 786440 | tf_op jit(solution)/shard_map/ppermute | solution.py:39
  6.8 0.2 collective-permute-start.3
  7.0 2.6 %collective-permute-start.2 = (bf16[16,8192]{1,0:T(8,128)(2,1)}, bf16[16,8192]{1,0:T(8,128)(2,1)S(1)}, u32[]{:S(2)}, u32[]{:S(2)}) collective-permute-start(bf16[16,8192]{1,0:T(8,128)(2,1)} %bitcast.18), channel_id=1, source_target_pairs={{0,48},{8,40},{16,0},{24,56},{32,16},{40,8},{48,32},{56,24},{64,11... | collective-permute-start | bytes 786440 | tf_op jit(solution)/shard_map/ppermute | solution.py:35
  9.6 0.0 collective-permute-done.1.second.refs_2_
  9.6 2.3 %collective-permute-done.first.refs_1_ = bf16[16,8192]{1,0:T(8,128)(2,1)S(1)} collective-permute-done((bf16[16,8192]{1,0:T(8,128)(2,1)}, bf16[16,8192]{1,0:T(8,128)(2,1)S(1)}, u32[]{:S(2)}, u32[]{:S(2)}) %collective-permute-start) | collective-permute-done | bytes 262176 | tf_op jit(solution)/shard_map/ppermute | solution.py:35
  12.0 0.0 copy-start.1
  12.0 0.0 copy-start.2
  12.0 3.2 %collective-permute-start.5 = (bf16[16,8192]{1,0:T(8,128)(2,1)S(1)}, bf16[16,8192]{1,0:T(8,128)(2,1)S(1)}, u32[]{:S(2)}, u32[]{:S(2)}) collective-permute-start(bf16[16,8192]{1,0:T(8,128)(2,1)S(1)} %pick.2), channel_id=1, source_target_pairs={{0,48},{8,72},{16,0},{24,88},{32,16},{40,104},{48,32},{56,120},{64... | collective-permute-start | bytes 786440 | tf_op jit(solution)/shard_map/ppermute | solution.py:35
  15.2 0.0 collective-permute-done.3.refs_4_
  15.2 3.8 %collective-permute-start.11 = (bf16[16,8192]{1,0:T(8,128)(2,1)S(1)}, bf16[16,8192]{1,0:T(8,128)(2,1)S(1)}, u32[]{:S(2)}, u32[]{:S(2)}) collective-permute-start(bf16[16,8192]{1,0:T(8,128)(2,1)S(1)} %collective-permute-done.3.refs_4_), channel_id=1, source_target_pairs={{0,8},{8,0},{1,9},{9,1},{2,10},{10,2},{3,11},{11,3},{4,12},{12,4},... | collective-permute-start | bytes 786440 | tf_op jit(solution)/shard_map/ppermute | solution.py:39
  19.0 0.0 collective-permute-done.2.second.refs_3_
  19.0 0.5 collective-permute-start.10
  19.6 0.0 copy-start
  19.6 2.3 %collective-permute-start.6 = (bf16[16,8192]{1,0:T(8,128)(2,1)S(1)}, bf16[16,8192]{1,0:T(8,128)(2,1)S(1)}, u32[]{:S(2)}, u32[]{:S(2)}) collective-permute-start(bf16[16,8192]{1,0:T(8,128)(2,1)S(1)} %pick.3), channel_id=1, source_target_pairs={{0,32},{8,72},{16,48},{24,88},{32,0},{40,104},{48,16},{56,120},{64... | collective-permute-start | bytes 786440 | tf_op jit(solution)/shard_map/ppermute | solution.py:35
  21.9 0.0 collective-permute-done.7.refs_8_
  21.9 0.7 collective-permute-start.4
  22.6 0.0 collective-permute-done.11.refs_12_
  22.6 0.5 collective-permute-start.9
  23.2 0.0 collective-permute-done.10.refs_11_
  23.2 0.1 collective-permute-start.8
  23.3 0.0 collective-permute-done.5.refs_6_
  23.3 0.4 collective-permute-start.13
  23.7 3.0 %collective-permute-done.6.refs_7_ = bf16[16,8192]{1,0:T(8,128)(2,1)S(1)} collective-permute-done((bf16[16,8192]{1,0:T(8,128)(2,1)S(1)}, bf16[16,8192]{1,0:T(8,128)(2,1)S(1)}, u32[]{:S(2)}, u32[]{:S(2)}) %collective-permute-start.6) | collective-permute-done | bytes 262176 | tf_op jit(solution)/shard_map/ppermute | solution.py:35
  26.7 0.9 collective-permute-start.14
  27.6 1.6 %collective-permute-done.4.refs_5_ = bf16[16,8192]{1,0:T(8,128)(2,1)S(1)} collective-permute-done((bf16[16,8192]{1,0:T(8,128)(2,1)S(1)}, bf16[16,8192]{1,0:T(8,128)(2,1)S(1)}, u32[]{:S(2)}, u32[]{:S(2)}) %collective-permute-start.4) | collective-permute-done | bytes 262176 | tf_op jit(solution)/shard_map/ppermute | solution.py:35
  29.2 1.2 %collective-permute-start.12 = (bf16[16,8192]{1,0:T(8,128)(2,1)S(1)}, bf16[16,8192]{1,0:T(8,128)(2,1)S(1)}, u32[]{:S(2)}, u32[]{:S(2)}) collective-permute-start(bf16[16,8192]{1,0:T(8,128)(2,1)S(1)} %collective-permute-done.4.refs_5_), channel_id=1, source_target_pairs={{0,8},{8,0},{1,9},{9,1},{2,10},{10,2},{3,11},{11,3},{4,12},{12,4},... | collective-permute-start | bytes 786440 | tf_op jit(solution)/shard_map/ppermute | solution.py:39
  30.4 0.0 copy-done.1
  30.4 2.5 %prepare.1 = (bf16[512,8192]{1,0:T(8,128)(2,1)S(1)}, f32[2,2,8,512]{3,2,1,0:T(8,128)S(1)}) custom-call(s32[64,512]{1,0:T(8,128)S(1)} %bitcast.20, bf16[2,512,128]{2,1,0:T(8,128)(2,1)S(1)} %copy-done.1), custom_call_target="tpu_custom_call" | custom-call | flops 4000000000 | bytes 12000000 | tf_op jit(solution)/shard_map/prepare/pallas_call | solution.py:82
  32.9 0.0 collective-permute-done.9.refs_10_
  32.9 0.0 collective-permute-done.8.refs_9_
  32.9 0.0 collective-permute-done.13.refs_14_
  33.0 0.0 collective-permute-done.14.refs_15_
  33.0 0.0 collective-permute-done.12.refs_13_
  33.0 0.0 slice-done
  33.0 0.0 slice-done.1
  33.0 0.0 slice-done.2
  33.0 0.0 copy-done
  33.0 0.0 slice-done.3
  33.0 0.0 copy-start.3
  33.0 4.6 %forward.1 = f32[8,2,2,8,512]{4,3,2,1,0:T(8,128)S(1)} custom-call(bf16[16,8192]{1,0:T(8,128)(2,1)S(1)} %bitcast.19, bf16[16,8192]{1,0:T(8,128)(2,1)S(1)} %collective-permute-done.first.refs_1_, bf16[16,8192]{1,0:T(8,128)(2,1)S(1)} %collective-permute-done.1.second.refs_2_, bf16[16,8192]{1,0:T(8,128)(2,1)S(1)} %collective-permute-done.2.second.refs_3_, ...), custom_call_target="tpu_custom_call" | custom-call | flops 6000000000 | bytes 18000000 | tf_op jit(solution)/shard_map/forward/pallas_call | solution.py:141
  37.7 15.6 %all_to_all.10.parts = f32[8,2,2,8,512]{4,3,2,1,0:T(8,128)S(1)} all-to-all(f32[8,2,2,8,512]{4,3,2,1,0:T(8,128)S(1)} %forward.1), channel_id=1, replica_groups=mesh['xh'=2,'y'=4,'c'=2,'z'=4,'xl'=2] {'z','xl'}, dimensions={0} | all-to-all | bytes 1048576 | tf_op jit(solution)/shard_map/all_to_all | solution.py:299
  53.2 0.7 residual.1
  53.9 8.6 %all_to_all.11.every_ref = bf16[8,2,2,8,512]{4,3,2,1,0:T(8,128)(2,1)S(1)} all-to-all(bf16[8,2,2,8,512]{4,3,2,1,0:T(8,128)(2,1)S(1)} %get-tuple-element.21), channel_id=1, replica_groups=mesh['xh'=2,'y'=4,'c'=2,'z'=4,'xl'=2] {'z','xl'}, dimensions={0} | all-to-all | bytes 524288 | tf_op jit(solution)/shard_map/all_to_all | solution.py:301
  62.5 2.4 %backward.3 = bf16[8,16,8192]{2,1,0:T(8,128)(2,1)S(1)} custom-call(bf16[8,2,2,8,512]{4,3,2,1,0:T(8,128)(2,1)S(1)} %all_to_all.11.every_ref, bf16[2,512,8192]{2,1,0:T(8,128)(2,1)S(1)} %bitcast.13, bf16[512,8192]{1,0:T(8,128)(2,1)S(1)} %get-tuple-element.18.refs_17_.wide_ref), custom_call_target="tpu_custom_call" | custom-call | flops 3000000000 | bytes 9000000 | tf_op jit(solution)/shard_map/backward/pallas_call | solution.py:205
  64.9 2.7 %collective-permute-start.15 = (bf16[8,16,8192]{2,1,0:T(8,128)(2,1)S(1)}, bf16[8,16,8192]{2,1,0:T(8,128)(2,1)S(1)}, u32[]{:S(2)}, u32[]{:S(2)}) collective-permute-start(bf16[8,16,8192]{2,1,0:T(8,128)(2,1)S(1)} %backward.3), channel_id=1, source_target_pairs={{0,8},{8,0},{1,9},{9,1},{2,10},{10,2},{3,11},{11,3},{4,12},{12,4},... | collective-permute-start | bytes 6291464 | tf_op jit(solution)/shard_map/ppermute | solution.py:39
  67.6 2.4 %backward.2 = (bf16[2,16,8192]{2,1,0:T(8,128)(2,1)S(1)}, bf16[2,16,8192]{2,1,0:T(8,128)(2,1)S(1)}, bf16[2,16,8192]{2,1,0:T(8,128)(2,1)S(1)}, bf16[2,16,8192]{2,1,0:T(8,128)(2,1)S(1)}) custom-call(bf16[8,2,2,8,512]{4,3,2,1,0:T(8,128)(2,1)S(1)} %all_to_all.11.every_ref, bf16[2,512,8192]{2,1,0:T(8,128)(2,1)S(1)} %bitcast.13, ...), custom_call_target="tpu_custom_call" | custom-call | flops 3000000000 | bytes 9000000 | tf_op jit(solution)/shard_map/backward/pallas_call | solution.py:205
  70.0 1.4 %collective-permute-done.15.came = bf16[8,16,8192]{2,1,0:T(8,128)(2,1)S(1)} collective-permute-done((bf16[8,16,8192]{2,1,0:T(8,128)(2,1)S(1)}, bf16[8,16,8192]{2,1,0:T(8,128)(2,1)S(1)}, u32[]{:S(2)}, u32[]{:S(2)}) %collective-permute-start.15) | collective-permute-done | bytes 2097184 | tf_op jit(solution)/shard_map/ppermute | solution.py:39
  71.4 0.5 chip_sum.1
  71.8 2.5 %collective-permute-start.16 = (bf16[2,16,8192]{2,1,0:T(8,128)(2,1)S(1)}, bf16[2,16,8192]{2,1,0:T(8,128)(2,1)S(1)}, u32[]{:S(2)}, u32[]{:S(2)}) collective-permute-start(bf16[2,16,8192]{2,1,0:T(8,128)(2,1)S(1)} %get-tuple-element.28), channel_id=1, source_target_pairs={{0,16},{8,72},{16,32},{24,88},{32,48},{40,104},{48,0},{56,120},{64... | collective-permute-start | bytes 1572872 | tf_op jit(solution)/shard_map/ppermute | solution.py:35
  74.4 0.5 collective-permute-start.17
  74.9 0.7 collective-permute-start.18
  75.6 5.9 %collective-permute-done.16.q1 = bf16[2,16,8192]{2,1,0:T(8,128)(2,1)S(1)} collective-permute-done((bf16[2,16,8192]{2,1,0:T(8,128)(2,1)S(1)}, bf16[2,16,8192]{2,1,0:T(8,128)(2,1)S(1)}, u32[]{:S(2)}, u32[]{:S(2)}) %collective-permute-start.16) | collective-permute-done | bytes 524320 | tf_op jit(solution)/shard_map/ppermute | solution.py:35
  81.4 5.9 %collective-permute-done.17.q2 = bf16[2,16,8192]{2,1,0:T(8,128)(2,1)S(1)} collective-permute-done((bf16[2,16,8192]{2,1,0:T(8,128)(2,1)S(1)}, bf16[2,16,8192]{2,1,0:T(8,128)(2,1)S(1)}, u32[]{:S(2)}, u32[]{:S(2)}) %collective-permute-start.17) | collective-permute-done | bytes 524320 | tf_op jit(solution)/shard_map/ppermute | solution.py:35
  87.4 0.0 collective-permute-done.18.q3
  87.4 0.2 stage_sum.1
  87.6 0.4 collective-permute-start.19
  88.0 4.3 %collective-permute-start.20 = (bf16[16,8192]{1,0:T(8,128)(2,1)S(1)}, bf16[16,8192]{1,0:T(8,128)(2,1)S(1)}, u32[]{:S(2)}, u32[]{:S(2)}) collective-permute-start(bf16[16,8192]{1,0:T(8,128)(2,1)S(1)} %get-tuple-element.32), channel_id=1, source_target_pairs={{8,56},{24,8},{40,24},{56,40},{72,120},{88,72},{104,88},{120,104},... | collective-permute-start | bytes 786440 | tf_op jit(solution)/shard_map/ppermute | solution.py:35
  92.2 2.2 %collective-permute-start.21 = (bf16[16,8192]{1,0:T(8,128)(2,1)S(1)}, bf16[16,8192]{1,0:T(8,128)(2,1)S(1)}, u32[]{:S(2)}, u32[]{:S(2)}) collective-permute-start(bf16[16,8192]{1,0:T(8,128)(2,1)S(1)} %get-tuple-element.33), channel_id=1, source_target_pairs={{8,40},{24,56},{40,8},{56,24},{72,104},{88,120},{104,72},{120,88},... | collective-permute-start | bytes 786440 | tf_op jit(solution)/shard_map/ppermute | solution.py:35
  94.4 0.0 collective-permute-done.19
  94.4 3.9 %collective-permute-done.20 = bf16[16,8192]{1,0:T(8,128)(2,1)S(1)} collective-permute-done((bf16[16,8192]{1,0:T(8,128)(2,1)S(1)}, bf16[16,8192]{1,0:T(8,128)(2,1)S(1)}, u32[]{:S(2)}, u32[]{:S(2)}) %collective-permute-start.20) | collective-permute-done | bytes 262176 | tf_op jit(solution)/shard_map/ppermute | solution.py:35
  98.3 2.5 %collective-permute-done.21 = bf16[16,8192]{1,0:T(8,128)(2,1)S(1)} collective-permute-done((bf16[16,8192]{1,0:T(8,128)(2,1)S(1)}, bf16[16,8192]{1,0:T(8,128)(2,1)S(1)}, u32[]{:S(2)}, u32[]{:S(2)}) %collective-permute-start.21) | collective-permute-done | bytes 262176 | tf_op jit(solution)/shard_map/ppermute | solution.py:35
  100.9 0.8 fusion
  (9 shorter events, 0.0 us)
Async XLA Ops:
  0.6 9.0 %collective-permute-start.1 = (bf16[16,8192]{1,0:T(8,128)(2,1)}, bf16[16,8192]{1,0:T(8,128)(2,1)S(1)}, u32[]{:S(2)}, u32[]{:S(2)}) collective-permute-start(bf16[16,8192]{1,0:T(8,128)(2,1)} %bitcast.14), channel_id=1, source_target_pairs={{0,16},{8,56},{16,32},{24,8},{32,48},{40,24},{48,0},{56,40},{64,80... | collective-permute-start | bytes 786440 | tf_op jit(solution)/shard_map/ppermute | solution.py:35
  4.2 7.7 %collective-permute-start = (bf16[16,8192]{1,0:T(8,128)(2,1)}, bf16[16,8192]{1,0:T(8,128)(2,1)S(1)}, u32[]{:S(2)}, u32[]{:S(2)}) collective-permute-start(bf16[16,8192]{1,0:T(8,128)(2,1)} %bitcast.15), channel_id=1, source_target_pairs={{0,64},{8,24},{16,80},{24,40},{32,96},{40,56},{48,112},{56,8},{64,... | collective-permute-start | bytes 786440 | tf_op jit(solution)/shard_map/ppermute | solution.py:35
  4.3 17.6 %collective-permute-start.7 = (bf16[16,8192]{1,0:T(8,128)(2,1)}, bf16[16,8192]{1,0:T(8,128)(2,1)S(1)}, u32[]{:S(2)}, u32[]{:S(2)}) collective-permute-start(bf16[16,8192]{1,0:T(8,128)(2,1)} %bitcast.16), channel_id=1, source_target_pairs={{0,8},{8,0},{1,9},{9,1},{2,10},{10,2},{3,11},{11,3},{4,12},{12,4},... | collective-permute-start | bytes 786440 | tf_op jit(solution)/shard_map/ppermute | solution.py:39
  6.8 8.4 %collective-permute-start.3 = (bf16[16,8192]{1,0:T(8,128)(2,1)}, bf16[16,8192]{1,0:T(8,128)(2,1)S(1)}, u32[]{:S(2)}, u32[]{:S(2)}) collective-permute-start(bf16[16,8192]{1,0:T(8,128)(2,1)} %bitcast.17), channel_id=1, source_target_pairs={{0,32},{8,72},{16,48},{24,88},{32,0},{40,104},{48,16},{56,120},{64... | collective-permute-start | bytes 786440 | tf_op jit(solution)/shard_map/ppermute | solution.py:35
  7.0 12.0 %collective-permute-start.2 = (bf16[16,8192]{1,0:T(8,128)(2,1)}, bf16[16,8192]{1,0:T(8,128)(2,1)S(1)}, u32[]{:S(2)}, u32[]{:S(2)}) collective-permute-start(bf16[16,8192]{1,0:T(8,128)(2,1)} %bitcast.18), channel_id=1, source_target_pairs={{0,48},{8,40},{16,0},{24,56},{32,16},{40,8},{48,32},{56,24},{64,11... | collective-permute-start | bytes 786440 | tf_op jit(solution)/shard_map/ppermute | solution.py:35
  12.0 18.4 %copy-start.1 = (bf16[2,512,128]{2,1,0:T(8,128)(2,1)S(1)}, bf16[2,512,128]{2,1,0:T(8,128)(2,1)}, u32[]{:S(2)}) copy-start(bf16[2,512,128]{2,1,0:T(8,128)(2,1)} %observed_ref.1) | copy-start | bytes 786436
  12.0 18.3 %copy-start.2 = (s32[512,64]{0,1:T(8,128)S(1)}, s32[512,64]{0,1:T(8,128)}, u32[]{:S(2)}) copy-start(s32[512,64]{0,1:T(8,128)} %param.6) | copy-start | bytes 393220
  12.0 11.2 %collective-permute-start.5 = (bf16[16,8192]{1,0:T(8,128)(2,1)S(1)}, bf16[16,8192]{1,0:T(8,128)(2,1)S(1)}, u32[]{:S(2)}, u32[]{:S(2)}) collective-permute-start(bf16[16,8192]{1,0:T(8,128)(2,1)S(1)} %pick.2), channel_id=1, source_target_pairs={{0,48},{8,72},{16,0},{24,88},{32,16},{40,104},{48,32},{56,120},{64... | collective-permute-start | bytes 786440 | tf_op jit(solution)/shard_map/ppermute | solution.py:35
  15.2 7.4 %collective-permute-start.11 = (bf16[16,8192]{1,0:T(8,128)(2,1)S(1)}, bf16[16,8192]{1,0:T(8,128)(2,1)S(1)}, u32[]{:S(2)}, u32[]{:S(2)}) collective-permute-start(bf16[16,8192]{1,0:T(8,128)(2,1)S(1)} %collective-permute-done.3.refs_4_), channel_id=1, source_target_pairs={{0,8},{8,0},{1,9},{9,1},{2,10},{10,2},{3,11},{11,3},{4,12},{12,4},... | collective-permute-start | bytes 786440 | tf_op jit(solution)/shard_map/ppermute | solution.py:39
  19.0 4.2 %collective-permute-start.10 = (bf16[16,8192]{1,0:T(8,128)(2,1)S(1)}, bf16[16,8192]{1,0:T(8,128)(2,1)S(1)}, u32[]{:S(2)}, u32[]{:S(2)}) collective-permute-start(bf16[16,8192]{1,0:T(8,128)(2,1)S(1)} %collective-permute-done.2.second.refs_3_), channel_id=1, source_target_pairs={{0,8},{8,0},{1,9},{9,1},{2,10},{10,2},{3,11},{11,3},{4,12},{12,4},... | collective-permute-start | bytes 786440 | tf_op jit(solution)/shard_map/ppermute | solution.py:39
  19.5 13.4 %slice-start = ((s8[16777216]{0:T(1024)(128)(4,1)}), s8[4194304]{0:T(1024)(128)(4,1)S(1)}, s32[]{:S(2)}) async-start(s8[16777216]{0:T(1024)(128)(4,1)} %bitcast.12), calls=%async_computation.2 | async-start | bytes 8388608
  19.5 13.5 %slice-start.1 = ((s8[16777216]{0:T(1024)(128)(4,1)}), s8[4194304]{0:T(1024)(128)(4,1)S(1)}, s32[]{:S(2)}) async-start(s8[16777216]{0:T(1024)(128)(4,1)} %bitcast.12), calls=%async_computation.3 | async-start | bytes 8388608
  19.5 13.5 %slice-start.2 = ((s8[16777216]{0:T(1024)(128)(4,1)}), s8[4194304]{0:T(1024)(128)(4,1)S(1)}, s32[]{:S(2)}) async-start(s8[16777216]{0:T(1024)(128)(4,1)} %bitcast.12), calls=%async_computation.4 | async-start | bytes 8388608
  19.6 13.5 %copy-start = (bf16[2,8192,8]{1,2,0:T(8,128)(2,1)S(1)}, bf16[2,8192,8]{1,2,0:T(8,128)(2,1)}, u32[]{:S(2)}) copy-start(bf16[2,8192,8]{1,2,0:T(8,128)(2,1)} %param.7) | copy-start | bytes 786436
  19.6 7.1 %collective-permute-start.6 = (bf16[16,8192]{1,0:T(8,128)(2,1)S(1)}, bf16[16,8192]{1,0:T(8,128)(2,1)S(1)}, u32[]{:S(2)}, u32[]{:S(2)}) collective-permute-start(bf16[16,8192]{1,0:T(8,128)(2,1)S(1)} %pick.3), channel_id=1, source_target_pairs={{0,32},{8,72},{16,48},{24,88},{32,0},{40,104},{48,16},{56,120},{64... | collective-permute-start | bytes 786440 | tf_op jit(solution)/shard_map/ppermute | solution.py:35
  21.9 7.3 %collective-permute-start.4 = (bf16[16,8192]{1,0:T(8,128)(2,1)S(1)}, bf16[16,8192]{1,0:T(8,128)(2,1)S(1)}, u32[]{:S(2)}, u32[]{:S(2)}) collective-permute-start(bf16[16,8192]{1,0:T(8,128)(2,1)S(1)} %collective-permute-done.first.refs_1_), channel_id=1, source_target_pairs={{0,16},{8,72},{16,32},{24,88},{32,48},{40,104},{48,0},{56,120},{64... | collective-permute-start | bytes 786440 | tf_op jit(solution)/shard_map/ppermute | solution.py:35
  22.6 10.3 %collective-permute-start.9 = (bf16[16,8192]{1,0:T(8,128)(2,1)S(1)}, bf16[16,8192]{1,0:T(8,128)(2,1)S(1)}, u32[]{:S(2)}, u32[]{:S(2)}) collective-permute-start(bf16[16,8192]{1,0:T(8,128)(2,1)S(1)} %collective-permute-done.1.second.refs_2_), channel_id=1, source_target_pairs={{0,8},{8,0},{1,9},{9,1},{2,10},{10,2},{3,11},{11,3},{4,12},{12,4},... | collective-permute-start | bytes 786440 | tf_op jit(solution)/shard_map/ppermute | solution.py:39
  23.2 9.8 %collective-permute-start.8 = (bf16[16,8192]{1,0:T(8,128)(2,1)S(1)}, bf16[16,8192]{1,0:T(8,128)(2,1)S(1)}, u32[]{:S(2)}, u32[]{:S(2)}) collective-permute-start(bf16[16,8192]{1,0:T(8,128)(2,1)S(1)} %collective-permute-done.first.refs_1_), channel_id=1, source_target_pairs={{0,8},{8,0},{1,9},{9,1},{2,10},{10,2},{3,11},{11,3},{4,12},{12,4},... | collective-permute-start | bytes 786440 | tf_op jit(solution)/shard_map/ppermute | solution.py:39
  23.3 9.7 %collective-permute-start.13 = (bf16[16,8192]{1,0:T(8,128)(2,1)S(1)}, bf16[16,8192]{1,0:T(8,128)(2,1)S(1)}, u32[]{:S(2)}, u32[]{:S(2)}) collective-permute-start(bf16[16,8192]{1,0:T(8,128)(2,1)S(1)} %collective-permute-done.5.refs_6_), channel_id=1, source_target_pairs={{0,8},{8,0},{1,9},{9,1},{2,10},{10,2},{3,11},{11,3},{4,12},{12,4},... | collective-permute-start | bytes 786440 | tf_op jit(solution)/shard_map/ppermute | solution.py:39
  26.7 6.3 %collective-permute-start.14 = (bf16[16,8192]{1,0:T(8,128)(2,1)S(1)}, bf16[16,8192]{1,0:T(8,128)(2,1)S(1)}, u32[]{:S(2)}, u32[]{:S(2)}) collective-permute-start(bf16[16,8192]{1,0:T(8,128)(2,1)S(1)} %collective-permute-done.6.refs_7_), channel_id=1, source_target_pairs={{0,8},{8,0},{1,9},{9,1},{2,10},{10,2},{3,11},{11,3},{4,12},{12,4},... | collective-permute-start | bytes 786440 | tf_op jit(solution)/shard_map/ppermute | solution.py:39
  29.2 3.8 %collective-permute-start.12 = (bf16[16,8192]{1,0:T(8,128)(2,1)S(1)}, bf16[16,8192]{1,0:T(8,128)(2,1)S(1)}, u32[]{:S(2)}, u32[]{:S(2)}) collective-permute-start(bf16[16,8192]{1,0:T(8,128)(2,1)S(1)} %collective-permute-done.4.refs_5_), channel_id=1, source_target_pairs={{0,8},{8,0},{1,9},{9,1},{2,10},{10,2},{3,11},{11,3},{4,12},{12,4},... | collective-permute-start | bytes 786440 | tf_op jit(solution)/shard_map/ppermute | solution.py:39
  30.4 2.6 %slice-start.3 = ((s8[16777216]{0:T(1024)(128)(4,1)}), s8[4194304]{0:T(1024)(128)(4,1)S(1)}, s32[]{:S(2)}) async-start(s8[16777216]{0:T(1024)(128)(4,1)} %bitcast.12), calls=%async_computation.5 | async-start | bytes 8388608
  33.0 20.2 %copy-start.3 = (s32[512]{0:T(512)S(1)}, s32[512]{0:T(512)}, u32[]{:S(2)}) copy-start(s32[512]{0:T(512)} %param.9) | copy-start | bytes 6148
  64.9 6.5 %collective-permute-start.15 = (bf16[8,16,8192]{2,1,0:T(8,128)(2,1)S(1)}, bf16[8,16,8192]{2,1,0:T(8,128)(2,1)S(1)}, u32[]{:S(2)}, u32[]{:S(2)}) collective-permute-start(bf16[8,16,8192]{2,1,0:T(8,128)(2,1)S(1)} %backward.3), channel_id=1, source_target_pairs={{0,8},{8,0},{1,9},{9,1},{2,10},{10,2},{3,11},{11,3},{4,12},{12,4},... | collective-permute-start | bytes 6291464 | tf_op jit(solution)/shard_map/ppermute | solution.py:39
  71.8 9.6 %collective-permute-start.16 = (bf16[2,16,8192]{2,1,0:T(8,128)(2,1)S(1)}, bf16[2,16,8192]{2,1,0:T(8,128)(2,1)S(1)}, u32[]{:S(2)}, u32[]{:S(2)}) collective-permute-start(bf16[2,16,8192]{2,1,0:T(8,128)(2,1)S(1)} %get-tuple-element.28), channel_id=1, source_target_pairs={{0,16},{8,72},{16,32},{24,88},{32,48},{40,104},{48,0},{56,120},{64... | collective-permute-start | bytes 1572872 | tf_op jit(solution)/shard_map/ppermute | solution.py:35
  74.4 13.0 %collective-permute-start.17 = (bf16[2,16,8192]{2,1,0:T(8,128)(2,1)S(1)}, bf16[2,16,8192]{2,1,0:T(8,128)(2,1)S(1)}, u32[]{:S(2)}, u32[]{:S(2)}) collective-permute-start(bf16[2,16,8192]{2,1,0:T(8,128)(2,1)S(1)} %get-tuple-element.29), channel_id=1, source_target_pairs={{0,48},{8,72},{16,0},{24,88},{32,16},{40,104},{48,32},{56,120},{64... | collective-permute-start | bytes 1572872 | tf_op jit(solution)/shard_map/ppermute | solution.py:35
  74.9 12.5 %collective-permute-start.18 = (bf16[2,16,8192]{2,1,0:T(8,128)(2,1)S(1)}, bf16[2,16,8192]{2,1,0:T(8,128)(2,1)S(1)}, u32[]{:S(2)}, u32[]{:S(2)}) collective-permute-start(bf16[2,16,8192]{2,1,0:T(8,128)(2,1)S(1)} %get-tuple-element.26.u3), channel_id=1, source_target_pairs={{0,32},{16,48},{32,0},{48,16},{64,96},{80,112},{96,64},{112,80},{1... | collective-permute-start | bytes 1572872 | tf_op jit(solution)/shard_map/ppermute | solution.py:35
  87.6 6.8 %collective-permute-start.19 = (bf16[16,8192]{1,0:T(8,128)(2,1)S(1)}, bf16[16,8192]{1,0:T(8,128)(2,1)S(1)}, u32[]{:S(2)}, u32[]{:S(2)}) collective-permute-start(bf16[16,8192]{1,0:T(8,128)(2,1)S(1)} %get-tuple-element.31), channel_id=1, source_target_pairs={{0,64},{8,24},{16,80},{24,40},{32,96},{40,56},{48,112},{56,8},{64,... | collective-permute-start | bytes 786440 | tf_op jit(solution)/shard_map/ppermute | solution.py:35
  88.0 10.4 %collective-permute-start.20 = (bf16[16,8192]{1,0:T(8,128)(2,1)S(1)}, bf16[16,8192]{1,0:T(8,128)(2,1)S(1)}, u32[]{:S(2)}, u32[]{:S(2)}) collective-permute-start(bf16[16,8192]{1,0:T(8,128)(2,1)S(1)} %get-tuple-element.32), channel_id=1, source_target_pairs={{8,56},{24,8},{40,24},{56,40},{72,120},{88,72},{104,88},{120,104},... | collective-permute-start | bytes 786440 | tf_op jit(solution)/shard_map/ppermute | solution.py:35
  92.2 8.6 %collective-permute-start.21 = (bf16[16,8192]{1,0:T(8,128)(2,1)S(1)}, bf16[16,8192]{1,0:T(8,128)(2,1)S(1)}, u32[]{:S(2)}, u32[]{:S(2)}) collective-permute-start(bf16[16,8192]{1,0:T(8,128)(2,1)S(1)} %get-tuple-element.33), channel_id=1, source_target_pairs={{8,40},{24,56},{40,8},{56,24},{72,104},{88,120},{104,72},{120,88},... | collective-permute-start | bytes 786440 | tf_op jit(solution)/shard_map/ppermute | solution.py:35
